TPU v7x, 256 devices: a whole 4x4x8 slice. The times are simulated.
256 devices in a mesh: section: 4 (over y), task: 4 (over x), mp: 16 (over z, core).
Axes of the slice: x: 4, y: 4, z: 8, core: 2. Of those that a mesh axis runs over, the one named last changes fastest.
Arguments:
- hidden_in: bfloat16 [4, 256, 3584], P('task', 'mp'), may hold values from -6 to 6
- lengths: int32 [4], P('task'), may hold values from 128 to 256
- layer_targets: bfloat16 [4, 4, 256, 3584], P('section', 'task', 'mp'), may hold values from -27 to 27
- task_weights: float32 [4], replicated, may hold values from 0.25 to 1
- norm_gains: float32 [4, 2, 3584], P('section'), may hold values from 0.5 to 1.5
- query_weight: bfloat16 [4, 4, 3584, 4096], P('task', 'section', None, 'mp'), may hold values from -0.40089186 to 0.40089186
- key_weight: bfloat16 [4, 4, 3584, 2048], P('task', 'section', None, 'mp'), may hold values from -0.40089186 to 0.40089186
- value_weight: bfloat16 [4, 4, 3584, 2048], P('task', 'section', None, 'mp'), may hold values from -0.09375 to 0.09375
- output_weight: bfloat16 [4, 4, 4096, 3584], P('task', 'section', 'mp'), may hold values from -0.09375 to 0.09375
- query_fisher: bfloat16 [4, 4, 3584, 4096], P('task', 'section', None, 'mp'), may hold values from 0.0099487305 to 10
- key_fisher: bfloat16 [4, 4, 3584, 2048], P('task', 'section', None, 'mp'), may hold values from 0.0099487305 to 10
- value_fisher: bfloat16 [4, 4, 3584, 2048], P('task', 'section', None, 'mp'), may hold values from 0.0099487305 to 10
- output_fisher: bfloat16 [4, 4, 4096, 3584], P('task', 'section', 'mp'), may hold values from 0.0099487305 to 10
Outputs:
- hidden_out: bfloat16 [4, 4, 256, 3584], P('section', 'task', 'mp')
- losses: float32 [4, 4], P('section', 'task')
All inputs are finite; a program needn't handle non-finite values.
Results may differ from a plain program's by a relative error of at most 0.04.
Values may be sent and summed in bfloat16 or wider, within the bound.
No kernel may reach another device: no remote copies, remote signals or barrier semaphores. Data moves between devices by JAX's collectives and lax.ppermute only.
A program may use at most 128 MiB of HBM per device.

v0:
```python
import jax
import jax.numpy as jnp
from jax import lax
from jax.sharding import PartitionSpec as P

HEAD_DIM = 256


def in_one_piece(arrays, axis, dim, along):
    ends, at = ([], 0)
    for a in arrays[:-1]:
        at += a.shape[along]
        ends.append(at)
    both = jnp.concatenate(arrays, axis=along)
    return tuple(
        jnp.split(lax.psum_scatter(both, axis, scatter_dimension=dim, tiled=True), ends, axis=along)
    )


def rows_first(arrays, axis, dims):
    turned = [jnp.moveaxis(a, dim, 0) for a, dim in zip(arrays, dims)]
    widths = [t[0].size for t in turned]
    both = jnp.concatenate([t.reshape(-1, w) for t, w in zip(turned, widths)], axis=1)
    whole = lax.all_gather(both, axis, axis=0, tiled=True)
    pieces = jnp.split(whole, [sum(widths[:k]) for k in range(1, len(widths))], axis=1)
    return tuple(
        (
            jnp.moveaxis(b.reshape(-1, *t.shape[1:]), 0, dim)
            for b, t, dim in zip(pieces, turned, dims)
        )
    )


def laid_out(pieces, dim):
    lengths = list(pieces.shape[1:])
    lengths[dim] *= pieces.shape[0]
    return jnp.moveaxis(pieces, 0, dim).reshape(lengths)


def from_everyone(array, axis):
    copies = jnp.broadcast_to(array, (lax.axis_size(axis), *array.shape))
    return lax.all_to_all(copies, axis, split_axis=0, concat_axis=0, tiled=True)


def gather_directly(array, axis, dim):
    return laid_out(from_everyone(array, axis), dim)


def from_partner(array, axis, stride):
    return lax.ppermute(array, axis, [(i, i ^ 1 << stride) for i in range(lax.axis_size(axis))])


def in_blocks(array, dim, length):
    lengths = array.shape
    pieces = array.reshape(*lengths[:dim], length, lengths[dim] // length, *lengths[dim + 1 :])
    return jnp.moveaxis(pieces, dim, 0)


def summed_on_arrival(array, axis, dim):
    length = lax.axis_size(axis)
    pieces = lax.all_to_all(in_blocks(array, dim, length), axis, 0, 0, tiled=True)
    return jnp.sum(pieces.astype(jnp.float32), axis=0)


def taken_together(array, axis):
    return from_everyone(array, axis).sum(axis=0)


def shifted(value, axis, steps):
    count = lax.axis_size(axis)
    first, last = (max(0, -steps), min(count, count - steps))
    return lax.ppermute(value, axis, [(source, source + steps) for source in range(first, last)])


def normalize(values, gain_row):
    widened = values.astype(jnp.float32)
    return (
        widened * lax.rsqrt(jnp.mean(widened * widened, axis=-1, keepdims=True) + 1e-06) * gain_row
    )


def rotate(values):
    half_width = values.shape[-1] // 2
    frequency = 10000.0 ** (-2.0 * jnp.arange(half_width, dtype=jnp.float32) / values.shape[-1])
    angles = jnp.arange(values.shape[0], dtype=jnp.float32)[:, None] * frequency[None, :]
    cosine = jnp.cos(angles)[:, None, :]
    sine_wave = jnp.sin(angles)[:, None, :]
    first_half = values[..., :half_width]
    second_half = values[..., half_width:]
    return jnp.concatenate(
        [
            first_half * cosine - second_half * sine_wave,
            second_half * cosine + first_half * sine_wave,
        ],
        axis=-1,
    )


def complete(own_part, peer_part, lower_half):
    return jnp.where(
        lower_half,
        jnp.concatenate([own_part, peer_part], axis=-1),
        jnp.concatenate([peer_part, own_part], axis=-1),
    )


def attend(queries, key_rows, value_rows, length):
    seq_len, head_count, head_width = queries.shape
    block_rows = min(seq_len, 512)
    key_positions = jnp.arange(seq_len, dtype=jnp.int32)

    def one_block(items):
        query_block, row_start = items
        scores = jnp.einsum(
            "qhd,khd->hqk", query_block, key_rows, preferred_element_type=jnp.float32
        ) * head_width ** (-0.5)
        capped = 50.0 * jnp.tanh(scores / 50.0)
        query_positions = row_start + jnp.arange(block_rows, dtype=jnp.int32)
        allowed = (key_positions[None, :] <= query_positions[:, None]) & (
            key_positions[None, :] < length
        )
        numerators = jnp.where(allowed[None], jnp.exp(capped), 0.0)
        probs = (numerators / jnp.sum(numerators, axis=-1, keepdims=True)).astype(jnp.bfloat16)
        return jnp.einsum(
            "hqk,khd->qhd", probs, value_rows, preferred_element_type=jnp.float32
        ).astype(jnp.bfloat16)

    blocks = queries.reshape(seq_len // block_rows, block_rows, head_count, head_width)
    starts = jnp.arange(seq_len // block_rows, dtype=jnp.int32) * block_rows
    context = lax.map(one_block, (blocks, starts))
    return context.reshape(seq_len, head_count * head_width)


def per_device(
    hidden_in,
    lengths,
    layer_targets,
    task_weights,
    norm_gains,
    query_weight,
    key_weight,
    value_weight,
    output_weight,
    query_fisher,
    key_fisher,
    value_fisher,
    output_fisher,
):
    task_scale = lax.dynamic_index_in_dim(task_weights, lax.axis_index("task"), 0, keepdims=False)
    query_scaled = query_fisher[0, 0].astype(jnp.float32) * task_scale
    key_scaled = key_fisher[0, 0].astype(jnp.float32) * task_scale
    value_scaled = value_fisher[0, 0].astype(jnp.float32) * task_scale
    output_scaled = output_fisher[0, 0].astype(jnp.float32) * task_scale
    query_terms = query_scaled * query_weight[0, 0].astype(jnp.float32)
    key_terms = key_scaled * key_weight[0, 0].astype(jnp.float32)
    value_terms = value_scaled * value_weight[0, 0].astype(jnp.float32)
    output_terms = output_scaled * output_weight[0, 0].astype(jnp.float32)
    reduced = (
        *tuple(
            (
                part.astype(jnp.float32)
                for part in in_one_piece(
                    (
                        query_terms.astype(jnp.bfloat16),
                        key_terms.astype(jnp.bfloat16),
                        value_terms.astype(jnp.bfloat16),
                    ),
                    "task",
                    0,
                    1,
                )
            )
        ),
        lax.psum_scatter(
            output_terms.astype(jnp.bfloat16), "task", scatter_dimension=1, tiled=True
        ).astype(jnp.float32),
        *tuple(
            (
                part.astype(jnp.float32)
                for part in in_one_piece(
                    (
                        query_scaled.astype(jnp.bfloat16),
                        key_scaled.astype(jnp.bfloat16),
                        value_scaled.astype(jnp.bfloat16),
                    ),
                    "task",
                    0,
                    1,
                )
            )
        ),
        lax.psum_scatter(
            output_scaled.astype(jnp.bfloat16), "task", scatter_dimension=1, tiled=True
        ).astype(jnp.float32),
    )
    shares = [(reduced[member] / reduced[member + 4]).astype(jnp.bfloat16) for member in range(4)]
    merged_query, merged_key, merged_value, merged_output = rows_first(
        (shares[0], shares[1], shares[2], shares[3]), "task", (0, 0, 0, 1)
    )
    mp_index = lax.axis_index("mp")
    lower_half = mp_index % 2 == 0
    projection = jnp.concatenate([merged_query, merged_key, merged_value], axis=1)
    query_cols = merged_query.shape[1]
    key_cols = merged_key.shape[1]
    gain_pair = norm_gains[0]
    targets_here = layer_targets[0]
    micro_count = hidden_in.shape[0]
    shard_rows = hidden_in.shape[1]
    width = hidden_in.shape[2]
    section_index = lax.axis_index("section")
    step_count = micro_count + lax.axis_size("section") - 1
    own_positions = mp_index * shard_rows + jnp.arange(shard_rows, dtype=jnp.int32)

    def layer(states, length, target):
        normed = normalize(states, gain_pair[0]).astype(jnp.bfloat16)
        projected = jnp.dot(
            gather_directly(normed, "mp", 0), projection, preferred_element_type=jnp.float32
        )
        seq_len = projected.shape[0]
        queries = rotate(projected[:, :query_cols].reshape(seq_len, -1, HEAD_DIM)).astype(
            jnp.bfloat16
        )
        key_raw = projected[:, query_cols : query_cols + key_cols].astype(jnp.bfloat16)
        value_raw = projected[:, query_cols + key_cols :].astype(jnp.bfloat16)
        peer_key, peer_value = from_partner((key_raw, value_raw), "mp", 0)
        key_raw = complete(key_raw, peer_key, lower_half)
        value_raw = complete(value_raw, peer_value, lower_half)
        key_rows = rotate(key_raw.astype(jnp.float32).reshape(seq_len, -1, HEAD_DIM)).astype(
            jnp.bfloat16
        )
        value_rows = value_raw.reshape(seq_len, -1, HEAD_DIM)
        group_size = queries.shape[1] // key_rows.shape[1]
        key_rows = jnp.repeat(key_rows, group_size, axis=1)
        value_rows = jnp.repeat(value_rows, group_size, axis=1)
        context = attend(queries, key_rows, value_rows, length)
        attention_out = summed_on_arrival(
            jnp.dot(context, merged_output, preferred_element_type=jnp.float32).astype(
                jnp.bfloat16
            ),
            "mp",
            0,
        )
        layer_out = (states.astype(jnp.float32) + normalize(attention_out, gain_pair[1])).astype(
            jnp.bfloat16
        )
        mismatch = layer_out.astype(jnp.float32) - target.astype(jnp.float32)
        live_rows = own_positions < length
        return (layer_out, jnp.sum(jnp.where(live_rows[:, None], mismatch * mismatch, 0.0)))

    def advance(step_index, carry):
        incoming, outputs, loss_parts = carry
        micro_index = step_index - section_index
        valid = (micro_index >= 0) & (micro_index < micro_count)
        chosen = jnp.clip(micro_index, 0, micro_count - 1)
        entry_rows = lax.dynamic_index_in_dim(hidden_in, chosen, 0, keepdims=False)
        states = jnp.where(section_index == 0, entry_rows, incoming)
        length = lax.dynamic_index_in_dim(lengths, chosen, 0, keepdims=False)
        target = lax.dynamic_index_in_dim(targets_here, chosen, 0, keepdims=False)
        layer_out, loss_part = layer(states, length, target)
        loss_value = taken_together(loss_part, "mp") / (length.astype(jnp.float32) * width)
        outputs = jnp.where(
            valid, lax.dynamic_update_index_in_dim(outputs, layer_out, chosen, 0), outputs
        )
        loss_parts = jnp.where(
            valid, lax.dynamic_update_index_in_dim(loss_parts, loss_value, chosen, 0), loss_parts
        )
        incoming = shifted(layer_out, "section", 1)
        return (incoming, outputs, loss_parts)

    start_carry = (
        jnp.zeros((shard_rows, width), jnp.bfloat16),
        jnp.zeros(hidden_in.shape, jnp.bfloat16),
        jnp.zeros((micro_count,), jnp.float32),
    )
    final_carry = lax.fori_loop(0, step_count, advance, start_carry)
    outputs = final_carry[1]
    loss_parts = final_carry[2]
    return (outputs[None], loss_parts[None])


def solution(mesh):
    in_specs = (
        P("task", "mp", None),
        P("task"),
        P("section", "task", "mp", None),
        P(),
        P("section", None, None),
        P("task", "section", None, "mp"),
        P("task", "section", None, "mp"),
        P("task", "section", None, "mp"),
        P("task", "section", "mp", None),
        P("task", "section", None, "mp"),
        P("task", "section", None, "mp"),
        P("task", "section", None, "mp"),
        P("task", "section", "mp", None),
    )
    out_specs = (P("section", "task", "mp", None), P("section", "task"))
    return jax.shard_map(
        per_device, mesh=mesh, in_specs=in_specs, out_specs=out_specs, check_vma=False
    )
```

profile of v0, /device:TPU:1, one launch (start us, length us, event | category | flops | bytes accessed | tf_op | source)
XLA Modules:
  0.0 762.2 jit_solution(9609427050068692780)
XLA Ops:
  8.5 4.5 fusion.50
  41.0 6.0 copy.44
  50.0 6.0 copy.46
  57.5 25.8 %reduce-scatter.19.cloned.1.call-done = bf16[896,256]{1,0:T(8,128)(2,1)} async-done(((bf16[3584,256]{1,0:T(8,128)(2,1)}), bf16[896,256]{1,0:T(8,128)(2,1)}) %reduce-scatter.19.cloned.1.call-update) | async-done | bytes 458768
  84.7 46.0 %reduce-scatter.13.cloned.1.call-done = bf16[896,512]{1,0:T(8,128)(2,1)} async-done(((bf16[3584,512]{1,0:T(8,128)(2,1)}), bf16[896,512]{1,0:T(8,128)(2,1)}) %reduce-scatter.13.cloned.1.call-update) | async-done | bytes 917520
  132.5 45.5 %reduce-scatter.15.cloned.1.call-done = bf16[896,512]{1,0:T(8,128)(2,1)} async-done(((bf16[3584,512]{1,0:T(8,128)(2,1)}), bf16[896,512]{1,0:T(8,128)(2,1)}) %reduce-scatter.15.cloned.1.call-update) | async-done | bytes 917520
  182.0 60.8 %all-gather.2.cloned.1.call-done = bf16[3584,768]{0,1:T(8,128)(2,1)} async-done(((bf16[896,768]{0,1:T(8,128)(2,1)}), bf16[3584,768]{0,1:T(8,128)(2,1)}) %all-gather.2.cloned.1.call-update) | async-done | bytes 5505040 | tf_op jit(solution)/shard_map/all_gather | solution.py:24
  242.8 4.2 split.40
  247.0 5.9 copy.43
  255.9 498.0 %while.28 = (s32[]{:T(128)}, bf16[16,3584]{1,0:T(8,128)(2,1)S(1)}, bf16[1,16,3584]{2,1,0:T(8,128)(2,1)S(1)}, f32[1]{0:T(128)}, pred[]{:T(512)}, /*index=5*/bf16[...) while((s32[]{:T(128)}, bf16[16,3584]{1,0:T(8,128)(2,1)S(1)}, ...), condition=%wide.region_11.12_spmd.clone, body=%wide.region_4.11_spmd.clone.sunk | while | flops 1483456768 | bytes 30745288 | solution.py:275
  257.7 7.7 %all-to-all-start = ((bf16[16,16,3584]{2,1,0:T(8,128)(2,1)}), bf16[16,16,3584]{2,1,0:T(8,128)(2,1)S(1)}, u32[]{:S(2)}, u32[]{:S(2)}) async-start(bf16[16,16,3584]{2,1,0:T(8,128)(2,1)} %broadcast_in_dim.156), calls=%async_computation | async-start | bytes 3670016 | tf_op jit(solution)/shard_map/while/body/eval_jaxpr/all_to_all | solution.py:42
  266.1 43.0 %all-to-all-done = bf16[16,16,3584]{2,1,0:T(8,128)(2,1)S(1)} async-done(((bf16[16,16,3584]{2,1,0:T(8,128)(2,1)}), bf16[16,16,3584]{2,1,0:T(8,128)(2,1)S(1)}, u32[]{:S(2)}, u32[]{:S(2)}) %all-to-all-start) | async-done | bytes 1835040 | tf_op jit(solution)/shard_map/while/body/eval_jaxpr/all_to_all | solution.py:42
  318.1 4.7 all-to-all-start.1
  323.4 43.0 %all-to-all-done.1 = bf16[16,16,3584]{2,1,0:T(8,128)(2,1)S(1)} async-done(((bf16[16,16,3584]{2,1,0:T(8,128)(2,1)}), bf16[16,16,3584]{2,1,0:T(8,128)(2,1)S(1)}, u32[]{:S(2)}, u32[]{:S(2)}) %all-to-all-start.1) | async-done | bytes 1835040 | tf_op jit(solution)/shard_map/while/body/eval_jaxpr/all_to_all | solution.py:61
  369.0 4.7 all-to-all-start.2
  383.7 5.1 all-to-all-start
  389.4 43.0 %all-to-all-done = bf16[16,16,3584]{2,1,0:T(8,128)(2,1)S(1)} async-done(((bf16[16,16,3584]{2,1,0:T(8,128)(2,1)}), bf16[16,16,3584]{2,1,0:T(8,128)(2,1)S(1)}, u32[]{:S(2)}, u32[]{:S(2)}) %all-to-all-start) | async-done | bytes 1835040 | tf_op jit(solution)/shard_map/while/body/eval_jaxpr/all_to_all | solution.py:42
  441.4 4.7 all-to-all-start.1
  446.8 43.0 %all-to-all-done.1 = bf16[16,16,3584]{2,1,0:T(8,128)(2,1)S(1)} async-done(((bf16[16,16,3584]{2,1,0:T(8,128)(2,1)}), bf16[16,16,3584]{2,1,0:T(8,128)(2,1)S(1)}, u32[]{:S(2)}, u32[]{:S(2)}) %all-to-all-start.1) | async-done | bytes 1835040 | tf_op jit(solution)/shard_map/while/body/eval_jaxpr/all_to_all | solution.py:61
  492.3 4.7 all-to-all-start.2
  507.0 6.0 all-to-all-start
  513.7 43.0 %all-to-all-done = bf16[16,16,3584]{2,1,0:T(8,128)(2,1)S(1)} async-done(((bf16[16,16,3584]{2,1,0:T(8,128)(2,1)}), bf16[16,16,3584]{2,1,0:T(8,128)(2,1)S(1)}, u32[]{:S(2)}, u32[]{:S(2)}) %all-to-all-start) | async-done | bytes 1835040 | tf_op jit(solution)/shard_map/while/body/eval_jaxpr/all_to_all | solution.py:42
  565.8 4.7 all-to-all-start.1
  571.1 43.0 %all-to-all-done.1 = bf16[16,16,3584]{2,1,0:T(8,128)(2,1)S(1)} async-done(((bf16[16,16,3584]{2,1,0:T(8,128)(2,1)}), bf16[16,16,3584]{2,1,0:T(8,128)(2,1)S(1)}, u32[]{:S(2)}, u32[]{:S(2)}) %all-to-all-start.1) | async-done | bytes 1835040 | tf_op jit(solution)/shard_map/while/body/eval_jaxpr/all_to_all | solution.py:61
  616.6 4.7 all-to-all-start.2
  621.3 4.1 collective-permute-start.2
  631.3 6.1 all-to-all-start
  638.0 43.0 %all-to-all-done = bf16[16,16,3584]{2,1,0:T(8,128)(2,1)S(1)} async-done(((bf16[16,16,3584]{2,1,0:T(8,128)(2,1)}), bf16[16,16,3584]{2,1,0:T(8,128)(2,1)S(1)}, u32[]{:S(2)}, u32[]{:S(2)}) %all-to-all-start) | async-done | bytes 1835040 | tf_op jit(solution)/shard_map/while/body/eval_jaxpr/all_to_all | solution.py:42
  690.1 4.7 all-to-all-start.1
  695.4 43.0 %all-to-all-done.1 = bf16[16,16,3584]{2,1,0:T(8,128)(2,1)S(1)} async-done(((bf16[16,16,3584]{2,1,0:T(8,128)(2,1)}), bf16[16,16,3584]{2,1,0:T(8,128)(2,1)S(1)}, u32[]{:S(2)}, u32[]{:S(2)}) %all-to-all-start.1) | async-done | bytes 1835040 | tf_op jit(solution)/shard_map/while/body/eval_jaxpr/all_to_all | solution.py:61
  740.9 4.7 all-to-all-start.2
  745.6 4.1 collective-permute-start.2
  (184 shorter events, 124.2 us)
Async XLA Ops:
  7.2 49.1 %reduce-scatter.17.cloned.1.call-start = ((), (), s32[]{:S(2)}) async-start(), calls=%async_computation.10 | async-start | bytes 2293760
  16.8 66.5 %reduce-scatter.19.cloned.1.call-start = ((), (), s32[]{:S(2)}) async-start(), calls=%async_computation.11 | async-start | bytes 2293760
  19.2 111.6 %reduce-scatter.13.cloned.1.call-start = ((), (), s32[]{:S(2)}) async-start(), calls=%async_computation.8 | async-start | bytes 4587520
  32.9 3.8 copy-start.1
  32.9 3.8 copy-start.2
  32.9 3.8 copy-start.3
  47.0 131.1 %reduce-scatter.15.cloned.1.call-start = ((), (), s32[]{:S(2)}) async-start(), calls=%async_computation.9 | async-start | bytes 4587520
  56.0 186.8 %all-gather.2.cloned.1.call-start = ((), (), s32[]{:S(2)}) async-start(), calls=%async_computation.7 | async-start | bytes 6881280 | tf_op jit(solution)/shard_map/all_gather | solution.py:24
  257.7 51.4 %all-to-all-start = ((bf16[16,16,3584]{2,1,0:T(8,128)(2,1)}), bf16[16,16,3584]{2,1,0:T(8,128)(2,1)S(1)}, u32[]{:S(2)}, u32[]{:S(2)}) async-start(bf16[16,16,3584]{2,1,0:T(8,128)(2,1)} %broadcast_in_dim.156), calls=%async_computation | async-start | bytes 3670016 | tf_op jit(solution)/shard_map/while/body/eval_jaxpr/all_to_all | solution.py:42
  312.2 1.3 collective-permute-start
  312.3 2.1 collective-permute-start.1
  318.1 48.3 %all-to-all-start.1 = ((bf16[16,16,3584]{2,1,0:T(8,128)(2,1)}), bf16[16,16,3584]{2,1,0:T(8,128)(2,1)S(1)}, u32[]{:S(2)}, u32[]{:S(2)}) async-start(bf16[16,16,3584]{2,1,0:T(8,128)(2,1)} %bitcast.94), calls=%async_computation.1 | async-start | bytes 3670016 | tf_op jit(solution)/shard_map/while/body/eval_jaxpr/all_to_all | solution.py:61
  369.0 11.6 %all-to-all-start.2 = ((f32[16,1,1]{2,1,0:T(1,128)}), f32[16,1,1]{2,1,0:T(1,128)S(1)}, u32[]{:S(2)}, u32[]{:S(2)}) async-start(f32[16,1,1]{2,1,0:T(1,128)} %broadcast_in_dim.157), calls=%async_computation.2 | async-start | bytes 16384 | tf_op jit(solution)/shard_map/while/body/eval_jaxpr/all_to_all | solution.py:42
  373.6 8.2 %collective-permute-start.2 = (bf16[16,3584]{1,0:T(8,128)(2,1)S(1)}, bf16[16,3584]{1,0:T(8,128)(2,1)S(1)}, u32[]{:S(2)}, u32[]{:S(2)}) collective-permute-start(bf16[16,3584]{1,0:T(8,128)(2,1)S(1)} %get-tuple-element.659), channel_id=1, source_target_pairs={{0,64},{64,128},{128,192},{1,65},{65,129},{129,193},{2,66},{66,130... | collective-permute-start | bytes 344072 | tf_op jit(solution)/shard_map/while/body/eval_jaxpr/ppermute | solution.py:72
  383.7 48.7 %all-to-all-start = ((bf16[16,16,3584]{2,1,0:T(8,128)(2,1)}), bf16[16,16,3584]{2,1,0:T(8,128)(2,1)S(1)}, u32[]{:S(2)}, u32[]{:S(2)}) async-start(bf16[16,16,3584]{2,1,0:T(8,128)(2,1)} %broadcast_in_dim.156), calls=%async_computation | async-start | bytes 3670016 | tf_op jit(solution)/shard_map/while/body/eval_jaxpr/all_to_all | solution.py:42
  435.6 1.3 collective-permute-start
  435.7 2.1 collective-permute-start.1
  441.4 48.3 %all-to-all-start.1 = ((bf16[16,16,3584]{2,1,0:T(8,128)(2,1)}), bf16[16,16,3584]{2,1,0:T(8,128)(2,1)S(1)}, u32[]{:S(2)}, u32[]{:S(2)}) async-start(bf16[16,16,3584]{2,1,0:T(8,128)(2,1)} %bitcast.94), calls=%async_computation.1 | async-start | bytes 3670016 | tf_op jit(solution)/shard_map/while/body/eval_jaxpr/all_to_all | solution.py:61
  492.3 11.6 %all-to-all-start.2 = ((f32[16,1,1]{2,1,0:T(1,128)}), f32[16,1,1]{2,1,0:T(1,128)S(1)}, u32[]{:S(2)}, u32[]{:S(2)}) async-start(f32[16,1,1]{2,1,0:T(1,128)} %broadcast_in_dim.157), calls=%async_computation.2 | async-start | bytes 16384 | tf_op jit(solution)/shard_map/while/body/eval_jaxpr/all_to_all | solution.py:42
  496.9 8.2 %collective-permute-start.2 = (bf16[16,3584]{1,0:T(8,128)(2,1)S(1)}, bf16[16,3584]{1,0:T(8,128)(2,1)S(1)}, u32[]{:S(2)}, u32[]{:S(2)}) collective-permute-start(bf16[16,3584]{1,0:T(8,128)(2,1)S(1)} %get-tuple-element.659), channel_id=1, source_target_pairs={{0,64},{64,128},{128,192},{1,65},{65,129},{129,193},{2,66},{66,130... | collective-permute-start | bytes 344072 | tf_op jit(solution)/shard_map/while/body/eval_jaxpr/ppermute | solution.py:72
  507.0 49.7 %all-to-all-start = ((bf16[16,16,3584]{2,1,0:T(8,128)(2,1)}), bf16[16,16,3584]{2,1,0:T(8,128)(2,1)S(1)}, u32[]{:S(2)}, u32[]{:S(2)}) async-start(bf16[16,16,3584]{2,1,0:T(8,128)(2,1)} %broadcast_in_dim.156), calls=%async_computation | async-start | bytes 3670016 | tf_op jit(solution)/shard_map/while/body/eval_jaxpr/all_to_all | solution.py:42
  559.9 1.3 collective-permute-start
  560.0 2.1 collective-permute-start.1
  565.8 48.3 %all-to-all-start.1 = ((bf16[16,16,3584]{2,1,0:T(8,128)(2,1)}), bf16[16,16,3584]{2,1,0:T(8,128)(2,1)S(1)}, u32[]{:S(2)}, u32[]{:S(2)}) async-start(bf16[16,16,3584]{2,1,0:T(8,128)(2,1)} %bitcast.94), calls=%async_computation.1 | async-start | bytes 3670016 | tf_op jit(solution)/shard_map/while/body/eval_jaxpr/all_to_all | solution.py:61
  616.6 11.6 %all-to-all-start.2 = ((f32[16,1,1]{2,1,0:T(1,128)}), f32[16,1,1]{2,1,0:T(1,128)S(1)}, u32[]{:S(2)}, u32[]{:S(2)}) async-start(f32[16,1,1]{2,1,0:T(1,128)} %broadcast_in_dim.157), calls=%async_computation.2 | async-start | bytes 16384 | tf_op jit(solution)/shard_map/while/body/eval_jaxpr/all_to_all | solution.py:42
  621.3 8.2 %collective-permute-start.2 = (bf16[16,3584]{1,0:T(8,128)(2,1)S(1)}, bf16[16,3584]{1,0:T(8,128)(2,1)S(1)}, u32[]{:S(2)}, u32[]{:S(2)}) collective-permute-start(bf16[16,3584]{1,0:T(8,128)(2,1)S(1)} %get-tuple-element.659), channel_id=1, source_target_pairs={{0,64},{64,128},{128,192},{1,65},{65,129},{129,193},{2,66},{66,130... | collective-permute-start | bytes 344072 | tf_op jit(solution)/shard_map/while/body/eval_jaxpr/ppermute | solution.py:72
  631.3 49.7 %all-to-all-start = ((bf16[16,16,3584]{2,1,0:T(8,128)(2,1)}), bf16[16,16,3584]{2,1,0:T(8,128)(2,1)S(1)}, u32[]{:S(2)}, u32[]{:S(2)}) async-start(bf16[16,16,3584]{2,1,0:T(8,128)(2,1)} %broadcast_in_dim.156), calls=%async_computation | async-start | bytes 3670016 | tf_op jit(solution)/shard_map/while/body/eval_jaxpr/all_to_all | solution.py:42
  684.2 1.3 collective-permute-start
  684.3 2.1 collective-permute-start.1
  690.1 48.3 %all-to-all-start.1 = ((bf16[16,16,3584]{2,1,0:T(8,128)(2,1)}), bf16[16,16,3584]{2,1,0:T(8,128)(2,1)S(1)}, u32[]{:S(2)}, u32[]{:S(2)}) async-start(bf16[16,16,3584]{2,1,0:T(8,128)(2,1)} %bitcast.94), calls=%async_computation.1 | async-start | bytes 3670016 | tf_op jit(solution)/shard_map/while/body/eval_jaxpr/all_to_all | solution.py:61
  740.9 11.6 %all-to-all-start.2 = ((f32[16,1,1]{2,1,0:T(1,128)}), f32[16,1,1]{2,1,0:T(1,128)S(1)}, u32[]{:S(2)}, u32[]{:S(2)}) async-start(f32[16,1,1]{2,1,0:T(1,128)} %broadcast_in_dim.157), calls=%async_computation.2 | async-start | bytes 16384 | tf_op jit(solution)/shard_map/while/body/eval_jaxpr/all_to_all | solution.py:42
  745.6 8.2 %collective-permute-start.2 = (bf16[16,3584]{1,0:T(8,128)(2,1)S(1)}, bf16[16,3584]{1,0:T(8,128)(2,1)S(1)}, u32[]{:S(2)}, u32[]{:S(2)}) collective-permute-start(bf16[16,3584]{1,0:T(8,128)(2,1)S(1)} %get-tuple-element.659), channel_id=1, source_target_pairs={{0,64},{64,128},{128,192},{1,65},{65,129},{129,193},{2,66},{66,130... | collective-permute-start | bytes 344072 | tf_op jit(solution)/shard_map/while/body/eval_jaxpr/ppermute | solution.py:72
  (11 other events, 26.8 us)
Sparse Core Ops, SparseCore 0:
  16.9 33.9 reduce-scatter.16
  53.4 29.8 reduce-scatter.18
  85.9 44.8 reduce-scatter.12
  133.2 44.8 reduce-scatter.14
  181.4 61.3 all-gather.1
where the time goes:
time: 764 us; the launch traced here: 762 us
  waiting for transfers between devices  537 us (70%)
  starting transfers between devices  80.4 us (11%)
  local copies, waits for them, and re-layouts  64 us (8%)
  other arithmetic  33.5 us (4%)
  matrix products  28.3 us (4%)
  between operations  15.8 us (2%)
    all_to_all x8, waiting for transfers between devices, from_everyone(): return lax.all_to_all(copies, axis, split_axis=0, concat_axis=0, tiled=True)  184 us
    all_to_all x4, waiting for transfers between devices, summed_on_arrival(): lax.all_to_all(in_blocks(array, dim, length), axis, 0, 0, tiled=True)  172 us
    unnamed x9, waiting for transfers between devices  117 us
    all_gather x1, waiting for transfers between devices, rows_first(): whole = lax.all_gather(both, axis, axis=0, tiled=True)  60.8 us
    all_to_all x8, starting transfers between devices, from_everyone(): return lax.all_to_all(copies, axis, split_axis=0, concat_axis=0, tiled=True)  43.5 us
    unnamed x43, local copies, waits for them, and re-layouts  41.9 us
    all_to_all x4, starting transfers between devices, summed_on_arrival(): lax.all_to_all(in_blocks(array, dim, length), axis, 0, 0, tiled=True)  18.6 us
    ppermute x4, starting transfers between devices, shifted(): lax.ppermute(value, axis, [(source, source + steps) for source in range(f...  15.5 us
  transfers between devices with their start and end apart: 29, of which 20 were waited for; matrix products, arithmetic and copies ran while one was open for 7% of the time, Pallas kernels for 0%

commit v1 on v0

v1 whole, which is shorter than its diff:
```python
import functools

import jax
import jax.numpy as jnp
from jax import lax
from jax.experimental import pallas as pl
from jax.experimental.pallas import tpu as pltpu
from jax.sharding import PartitionSpec as P

HEAD_DIM = 256
F32 = jnp.float32
BF16 = jnp.bfloat16
VMEM_BYTES = 56 * 1024 * 1024


def exchanged(array, axis, mask):
    return lax.ppermute(array, axis, [(i, i ^ mask) for i in range(lax.axis_size(axis))])


def params():
    return pltpu.CompilerParams(vmem_limit_bytes=VMEM_BYTES)


def share_call(idx, scale, weights, fishers, lane_block, blocks, count, received, finish):
    rows = weights[0].shape[1]
    sub = 224 if rows % 224 == 0 else rows
    widths = [w.shape[2] if lane_block is None else w.shape[2] // 2 for w in weights]
    lane = 0 if lane_block is None else lane_block
    total = sum(widths)
    n = len(weights)

    def own_map(j, r, s):
        return (s[blocks + j], r, lane)

    in_specs = [pl.BlockSpec(memory_space=pltpu.SMEM)]
    in_specs += [pl.BlockSpec((1, sub, w), own_map) for w in widths] * 2
    operands = [scale, *weights, *fishers]
    for array, entry in received:
        if entry is None:
            in_specs.append(pl.BlockSpec((2, 1, sub, total), lambda j, r, s: (0, 0, r, 0)))
        else:
            in_specs.append(
                pl.BlockSpec((2, 1, sub, total), lambda j, r, s, e=entry: (0, s[e], r, 0))
            )
        operands.append(array)

    def kernel(idx_ref, scale_ref, *refs):
        out_ref = refs[-1]
        task_scale = scale_ref[0]
        at = 0
        for k in range(n):
            scaled = refs[n + k][0].astype(F32) * task_scale
            term = scaled * refs[k][0].astype(F32)
            part = [term.astype(BF16), scaled.astype(BF16)]
            cols = slice(at, at + widths[k])
            at += widths[k]
            if received:
                part = [
                    p.astype(F32) + sum(g[i, 0, :, cols].astype(F32) for g in refs[2 * n : -1])
                    for i, p in enumerate(part)
                ]
            if finish:
                out_ref[:, cols] = (part[0] / part[1]).astype(BF16)
            else:
                out_ref[0, 0, :, cols] = part[0].astype(BF16)
                out_ref[1, 0, :, cols] = part[1].astype(BF16)

    if finish:
        out_shape = jax.ShapeDtypeStruct((rows, total), BF16)
        out_spec = pl.BlockSpec((sub, total), lambda j, r, s: (r, 0))
    else:
        out_shape = jax.ShapeDtypeStruct((2, count, rows, total), BF16)
        out_spec = pl.BlockSpec((2, 1, sub, total), lambda j, r, s: (0, j, r, 0))
    return pl.pallas_call(
        kernel,
        out_shape=out_shape,
        grid_spec=pltpu.PrefetchScalarGridSpec(
            num_scalar_prefetch=1,
            grid=(count, rows // sub),
            in_specs=in_specs,
            out_specs=out_spec,
        ),
        compiler_params=params(),
    )(idx, *operands)


def normed_copies(states, gain, copies):
    rows, width = states.shape

    def kernel(states_ref, gain_ref, out_ref):
        x = states_ref[...].astype(F32)
        scale = lax.rsqrt(jnp.mean(x * x, axis=-1, keepdims=True) + 1e-06)
        y = (x * scale * gain_ref[...]).astype(BF16)
        for k in range(copies):
            out_ref[k] = y

    return pl.pallas_call(
        kernel,
        out_shape=jax.ShapeDtypeStruct((copies, rows, width), BF16),
        compiler_params=params(),
    )(states, gain)


def project(idx, normed, own, peer, cosine, sine):
    copies, rows, width = normed.shape
    tokens = copies * rows
    quarter = width // 4
    half = own[2].shape[0]
    pieces = len(own)

    def kernel(idx_ref, x_ref, cos_ref, sin_ref, *refs):
        q_own_ref, q_peer_ref, kv_ref = refs[-3:]
        x_index = idx_ref[0]
        core = idx_ref[1]

        def one(ws):
            acc = None
            for d, lo, w in ws:
                at = pl.multiple_of((x_index ^ d) * quarter + lo, 128)
                part = x_ref[:, :, pl.ds(at, w.shape[0])].reshape(tokens, w.shape[0])
                prod = jnp.dot(part, w[...], preferred_element_type=F32)
                acc = prod if acc is None else acc + prod
            return acc

        def listed(ws):
            p0, p1, p2a, p2b, p3 = ws
            return [(0, 0, p0), (1, 0, p1), (2, 0, p2a), (2, half, p2b), (3, 0, p3)]

        mine = one(listed(refs[:pieces]))
        theirs = one(listed(refs[pieces : 2 * pieces]))
        cos = cos_ref[...]
        sin = sin_ref[...]

        def rotated(q):
            a = q[:, :128]
            b = q[:, 128:]
            return (a * cos - b * sin).astype(BF16), (b * cos + a * sin).astype(BF16)

        for ref, acc in ((q_own_ref, mine), (q_peer_ref, theirs)):
            lo, hi = rotated(acc[:, :256])
            ref[:, :128] = lo
            ref[:, 128:] = hi
        first = core == 0
        k_mine = mine[:, 256:384].astype(BF16).astype(F32)
        k_theirs = theirs[:, 256:384].astype(BF16).astype(F32)
        a = jnp.where(first, k_mine, k_theirs)
        b = jnp.where(first, k_theirs, k_mine)
        kv_ref[:, :128] = (a * cos - b * sin).astype(BF16)
        kv_ref[:, 128:256] = (b * cos + a * sin).astype(BF16)
        kv_ref[:, 256:384] = jnp.where(first, mine[:, 384:], theirs[:, 384:]).astype(BF16)
        kv_ref[:, 384:] = jnp.where(first, theirs[:, 384:], mine[:, 384:]).astype(BF16)

    vmem = pl.BlockSpec(memory_space=pltpu.VMEM)
    return pl.pallas_call(
        kernel,
        out_shape=(
            jax.ShapeDtypeStruct((tokens, 256), BF16),
            jax.ShapeDtypeStruct((tokens, 256), BF16),
            jax.ShapeDtypeStruct((tokens, 512), BF16),
        ),
        in_specs=[pl.BlockSpec(memory_space=pltpu.SMEM)] + [vmem] * (3 + 2 * pieces),
        out_specs=(vmem, vmem, vmem),
        compiler_params=params(),
    )(idx, normed, cosine, sine, *own, *peer)


def attend(idx, q_own, q_peer, kv_own, kv_peer, out_own, out_peer, copies):
    tokens = q_own.shape[0]
    rows = tokens // copies
    width = out_own.shape[1]

    def kernel(idx_ref, qo_ref, qp_ref, ko_ref, kp_ref, wo_ref, wp_ref, out_ref):
        core = idx_ref[1]
        length = idx_ref[2]

        def positions(shape, dim, which):
            i = lax.broadcasted_iota(jnp.int32, shape, dim)
            return (i // rows) * (2 * rows) + which * rows + i % rows

        shape = (tokens, tokens)
        q_pos = positions(shape, 0, core)
        masks = []
        for which in (core, 1 - core):
            k_pos = positions(shape, 1, which)
            masks.append((k_pos <= q_pos) & (k_pos < length))
        contexts = []
        for q_ref in (qo_ref, qp_ref):
            q = q_ref[...]
            numerators = []
            for kv_ref, allowed in ((ko_ref, masks[0]), (kp_ref, masks[1])):
                scores = lax.dot_general(
                    q,
                    kv_ref[:, :256],
                    (((1,), (1,)), ((), ())),
                    preferred_element_type=F32,
                ) * HEAD_DIM ** (-0.5)
                capped = 50.0 * jnp.tanh(scores / 50.0)
                numerators.append(jnp.where(allowed, jnp.exp(capped), 0.0))
            total = jnp.sum(numerators[0], axis=-1, keepdims=True) + jnp.sum(
                numerators[1], axis=-1, keepdims=True
            )
            ctx = None
            for num, kv_ref in zip(numerators, (ko_ref, kp_ref)):
                prod = jnp.dot(
                    (num / total).astype(BF16), kv_ref[:, 256:], preferred_element_type=F32
                )
                ctx = prod if ctx is None else ctx + prod
            contexts.append(ctx.astype(BF16))
        out = jnp.dot(contexts[0], wo_ref[...], preferred_element_type=F32) + jnp.dot(
            contexts[1], wp_ref[...], preferred_element_type=F32
        )
        out_ref[...] = out.astype(BF16).reshape(copies, rows, width)

    vmem = pl.BlockSpec(memory_space=pltpu.VMEM)
    return pl.pallas_call(
        kernel,
        out_shape=jax.ShapeDtypeStruct((copies, rows, width), BF16),
        in_specs=[pl.BlockSpec(memory_space=pltpu.SMEM)] + [vmem] * 6,
        out_specs=vmem,
        compiler_params=params(),
    )(idx, q_own, q_peer, kv_own, kv_peer, out_own, out_peer)


def assembled(idx, pieces):
    p0, p1, p2a, p2b, p3 = pieces
    rows, width = p0.shape
    half = p2a.shape[1]

    def kernel(idx_ref, r0, r1, r2a, r2b, r3, out_ref):
        x_index = idx_ref[0]
        out_ref[x_index] = r0[...]
        out_ref[x_index ^ 1] = r1[...]
        out_ref[x_index ^ 2, :, :half] = r2a[...]
        out_ref[x_index ^ 2, :, half:] = r2b[...]
        out_ref[x_index ^ 3] = r3[...]

    vmem = pl.BlockSpec(memory_space=pltpu.VMEM)
    return pl.pallas_call(
        kernel,
        out_shape=jax.ShapeDtypeStruct((4, rows, width), BF16),
        in_specs=[pl.BlockSpec(memory_space=pltpu.SMEM)] + [vmem] * 5,
        out_specs=vmem,
        compiler_params=params(),
    )(idx, p0, p1, p2a, p2b, p3).reshape(4 * rows, width)


def finished(pieces, states, gain):
    rows, width = states.shape

    def kernel(p_ref, states_ref, gain_ref, out_ref):
        total = jnp.sum(p_ref[...].astype(F32), axis=0)
        scale = lax.rsqrt(jnp.mean(total * total, axis=-1, keepdims=True) + 1e-06)
        out = states_ref[...].astype(F32) + total * scale * gain_ref[...]
        out_ref[...] = out.astype(BF16)

    return pl.pallas_call(
        kernel,
        out_shape=jax.ShapeDtypeStruct((rows, width), BF16),
        compiler_params=params(),
    )(pieces, states, gain)


def reduced_shares(plan, scale, sets):
    near, far = 1, 3
    halves = []
    for which, (weights, fishers, lane) in enumerate(sets):
        first, second = (near, far) if which == 0 else (far, near)
        base = 8 * which
        call = functools.partial(share_call, plan, scale, weights, fishers, lane)
        halves.append((call, base, first, second))
    got = [exchanged(call(base, 2, (), False), "task", first) for call, base, first, _ in halves]
    more = [
        exchanged(call(base + 2, 1, ((g, base + 3),), False), "task", second)
        for (call, base, _, second), g in zip(halves, got)
    ]
    return [
        call(base + 4, 1, ((g, base + 5), (m, None)), True)
        for (call, base, _, _), g, m in zip(halves, got, more)
    ]


def gathered_pieces(own, axis):
    dim, length = axis
    half = (length // 2 + 127) // 128 * 128
    from_near = exchanged(own, "task", 1)
    from_far = exchanged(own, "task", 3)
    low = lax.slice_in_dim(from_far, 0, half, axis=dim)
    high = lax.slice_in_dim(from_near, half, length, axis=dim)
    return (
        own,
        from_near,
        exchanged(low, "task", 1),
        exchanged(high, "task", 3),
        from_far,
    )


def per_device(
    hidden_in,
    lengths,
    layer_targets,
    task_weights,
    norm_gains,
    query_weight,
    key_weight,
    value_weight,
    output_weight,
    query_fisher,
    key_fisher,
    value_fisher,
    output_fisher,
):
    x_index = lax.axis_index("task")
    mp_index = lax.axis_index("mp")
    section_index = lax.axis_index("section")
    core = mp_index % 2
    chips = lax.axis_size("mp") // 2
    groups = [[2 * z + c for z in range(chips)] for c in range(2)]
    sections = lax.axis_size("section")
    states = hidden_in[0]
    rows, width = states.shape
    length = lengths[0]
    pre_gain = norm_gains[0, 0:1]
    post_gain = norm_gains[0, 1:2]
    scale = lax.dynamic_slice_in_dim(task_weights, x_index, 1)

    b = x_index // 2
    a = (x_index % 2) ^ b

    def block_a(h1, h2):
        return jnp.where(h1 == 0, 3 * h2, 1 + h2)

    def block_b(h1, h2):
        return jnp.where(h1 == 0, h2, 3 - h2)

    zero = jnp.zeros_like(a)
    plan = jnp.stack(
        [
            block_a(1 - a, 0),
            block_a(1 - a, 1),
            block_a(a, 1 - b),
            1 - b,
            x_index,
            b,
            zero,
            zero,
            block_b(1 - b, 0),
            block_b(1 - b, 1),
            block_b(b, 1 - a),
            1 - a,
            x_index,
            a,
            zero,
            zero,
        ]
    ).astype(jnp.int32)
    scalars = jnp.stack([x_index, core, length]).astype(jnp.int32)

    def quarters(array):
        array = array[0, 0]
        return array.reshape(4, array.shape[0] // 4, array.shape[1])

    qkv_sets = (
        ((quarters(query_weight),), (quarters(query_fisher),), None),
        (
            (quarters(key_weight), quarters(value_weight)),
            (quarters(key_fisher), quarters(value_fisher)),
            None,
        ),
    )
    out_sets = tuple(
        ((quarters(output_weight),), (quarters(output_fisher),), lane) for lane in (0, 1)
    )

    positions = (
        2 * rows * jnp.arange(chips, dtype=jnp.int32)[:, None]
        + core * rows
        + jnp.arange(rows, dtype=jnp.int32)[None, :]
    ).reshape(-1)
    frequency = 10000.0 ** (-2.0 * jnp.arange(HEAD_DIM // 2, dtype=F32) / HEAD_DIM)
    angles = positions.astype(F32)[:, None] * frequency[None, :]
    cosine = jnp.cos(angles)
    sine = jnp.sin(angles)

    def spread(array):
        return lax.all_to_all(array, "mp", 0, 0, tiled=True, axis_index_groups=groups)

    with jax.named_scope("merge_qkv"):
        q_share, kv_share = reduced_shares(plan, scale, qkv_sets)
        share = jnp.concatenate([q_share, kv_share], axis=1)
        qkv_own = gathered_pieces(share, (0, share.shape[0]))
        qkv_peer = tuple(exchanged(p, "mp", 1) for p in qkv_own)
    with jax.named_scope("merge_out"):
        low_share, high_share = reduced_shares(plan, scale, out_sets)
        share = jnp.concatenate([low_share, high_share], axis=1)
        out_own = assembled(scalars, gathered_pieces(share, (1, share.shape[1])))
        out_peer = exchanged(out_own, "mp", 1)

    chosen = None
    for step in range(sections):
        with jax.named_scope("layer"):
            if step > 0:
                states = lax.ppermute(
                    layer_out, "section", [(i, i + 1) for i in range(sections - 1)]
                )
            normed = spread(normed_copies(states, pre_gain, chips))
            q_own, q_peer, kv_own = project(scalars, normed, qkv_own, qkv_peer, cosine, sine)
            kv_peer = exchanged(kv_own, "mp", 1)
            partial = attend(scalars, q_own, q_peer, kv_own, kv_peer, out_own, out_peer, chips)
            layer_out = finished(spread(partial), states, post_gain)
            chosen = (
                layer_out
                if chosen is None
                else jnp.where(section_index == step, layer_out, chosen)
            )
    with jax.named_scope("loss"):
        own_positions = mp_index * rows + jnp.arange(rows, dtype=jnp.int32)
        mismatch = chosen.astype(F32) - layer_targets[0, 0].astype(F32)
        loss_part = jnp.sum(jnp.where((own_positions < length)[:, None], mismatch * mismatch, 0.0))
        copies = jnp.broadcast_to(loss_part, (2 * chips, 1))
        total = jnp.sum(lax.all_to_all(copies, "mp", 0, 0, tiled=True))
        loss = total / (length.astype(F32) * width)
    return (chosen[None, None], loss[None, None])


def solution(mesh):
    in_specs = (
        P("task", "mp", None),
        P("task"),
        P("section", "task", "mp", None),
        P(),
        P("section", None, None),
        P("task", "section", None, "mp"),
        P("task", "section", None, "mp"),
        P("task", "section", None, "mp"),
        P("task", "section", "mp", None),
        P("task", "section", None, "mp"),
        P("task", "section", None, "mp"),
        P("task", "section", None, "mp"),
        P("task", "section", "mp", None),
    )
    out_specs = (P("section", "task", "mp", None), P("section", "task"))
    return jax.shard_map(
        per_device, mesh=mesh, in_specs=in_specs, out_specs=out_specs, check_vma=False
    )
```

time: 764 us -> 534 us (0.70)
  waiting for transfers between devices: 537 us -> 146 us
  blocking collectives: 0 us -> 180 us
  Pallas kernels: 0 us -> 114 us
  local copies, waits for them, and re-layouts: 64 us -> 21.2 us
  other arithmetic: 33.5 us -> 4.79 us
  matrix products: 28.3 us -> 0 us
  starting transfers between devices: 80.4 us -> 62 us
  between operations: 15.8 us -> 3.4 us
    all_to_all x12 -> x3, waiting for transfers between devices: 356 us -> 31 us  [the longest x2 24 us: spread(): lax.all_to_all(array, 'mp', 0, 0, tiled=True, axis_index_groups=groups)]
    all_to_all x0 -> x6, blocking collectives: none -> 180 us  [spread(): lax.all_to_all(array, 'mp', 0, 0, tiled=True, axis_index_groups=groups)]
    unnamed x9 -> x0, waiting for transfers between devices: 117 us -> none
    pallas_call x0 -> x29, Pallas kernels: none -> 114 us  [the longest x12 55.6 us: share_call(): pl.pallas_call(kernel, out_shape=out_shape, grid_spec=pltpu.PrefetchScala...]
    ppermute x12 -> x29, waiting for transfers between devices: 2.91 us -> 115 us  [the longest x26 108 us: exchanged(): lax.ppermute(array, axis, [(i, i ^ mask) for i in range(lax.axis_size(axi...]
    all_gather x1 -> x0, waiting for transfers between devices: 60.8 us -> none  [rows_first(): whole = lax.all_gather(both, axis, axis=0, tiled=True)]
    all_to_all x12 -> x3, starting transfers between devices: 62.1 us -> 18.2 us  [the longest x2 12.1 us: spread(): lax.all_to_all(array, 'mp', 0, 0, tiled=True, axis_index_groups=groups)]
    unnamed x43 -> x64, local copies, waits for them, and re-layouts: 41.9 us -> 13.6 us
  transfers between devices with their start and end apart: 29 -> 32, of which waited for: 20 -> 20; matrix products, arithmetic and copies ran while one was open for 7% -> 1% of each run, Pallas kernels for 0% -> 11%
where the time goes in v1:
time: 534 us; the launch traced here: 531 us
  blocking collectives  180 us (34%)
  waiting for transfers between devices  146 us (27%)
  Pallas kernels  114 us (21%)
  starting transfers between devices  62 us (12%)
  local copies, waits for them, and re-layouts  21.2 us (4%)
    all_to_all x6, blocking collectives, spread(): lax.all_to_all(array, 'mp', 0, 0, tiled=True, axis_index_groups=groups)  180 us
    ppermute x26, waiting for transfers between devices, exchanged(): lax.ppermute(array, axis, [(i, i ^ mask) for i in range(lax.axis_size(axi...  108 us
    pallas_call x12, Pallas kernels, share_call(): pl.pallas_call(kernel, out_shape=out_shape, grid_spec=pltpu.PrefetchScala...  55.6 us
    ppermute x26, starting transfers between devices, exchanged(): lax.ppermute(array, axis, [(i, i ^ mask) for i in range(lax.axis_size(axi...  33 us
    all_to_all x2, waiting for transfers between devices, spread(): lax.all_to_all(array, 'mp', 0, 0, tiled=True, axis_index_groups=groups)  24 us
    pallas_call x4, Pallas kernels, project(): pl.pallas_call(kernel, out_shape=(jax.ShapeDtypeStruct((tokens, 256), BF1...  21.5 us
    pallas_call x4, Pallas kernels, attend(): pl.pallas_call(kernel, out_shape=jax.ShapeDtypeStruct((copies, rows, widt...  17.8 us
    unnamed x64, local copies, waits for them, and re-layouts  13.6 us
  transfers between devices with their start and end apart: 32, of which 20 were waited for; matrix products, arithmetic and copies ran while one was open for 1% of the time, Pallas kernels for 11%

profile of v1, /device:TPU:1, one launch (start us, length us, event | category | flops | bytes accessed | tf_op | source)
XLA Modules:
  0.0 531.0 jit_solution(7351745218931031811)
XLA Ops:
  2.6 7.0 %merge_qkv.6 = bf16[2,2,896,256]{3,2,1,0:T(8,128)(2,1)} custom-call(s32[16]{0:T(128)} %stack.57.idx_ref, f32[1]{0:T(128)} %dynamic_slice.3.scale_ref, bf16[4,896,256]{2,1,0:T(8,128)(2,1)} %bitcast.51, bf16[4,896,256]{2,1,0:T(8,128)(2,1)} %bitcast.54), custom_call_target="tpu_custom_call" | custom-call | tf_op jit(solution)/shard_map/merge_qkv/pallas_call | solution.py:74
  11.7 6.9 %merge_qkv.9 = bf16[2,2,896,256]{3,2,1,0:T(8,128)(2,1)} custom-call(s32[16]{0:T(128)} %stack.57.idx_ref, f32[1]{0:T(128)} %dynamic_slice.3.scale_ref, bf16[4,896,128]{2,1,0:T(8,128)(2,1)} %bitcast.57, bf16[4,896,128]{2,1,0:T(8,128)(2,1)} %bitcast.60, bf16[4,896,128]{2,1,0:T(8,128)(2,1)} %bitcast.63, bf16[4,896,128]{2,1,0:T(8,128)(2,1)} %bitcast.66), custom_call_target="tpu_custom_call" | custom-call | tf_op jit(solution)/shard_map/merge_qkv/pallas_call | solution.py:74
  28.2 41.8 %collective-permute-done.14.refs_2_ = bf16[2,2,64,1792]{3,2,1,0:T(8,128)(2,1)S(1)} collective-permute-done((bf16[2,2,64,1792]{3,2,1,0:T(8,128)(2,1)}, bf16[2,2,64,1792]{3,2,1,0:T(8,128)(2,1)S(1)}, u32[]{:S(2)}, u32[]{:S(2)}) %collective-permute-start.14) | collective-permute-done | bytes 917536 | tf_op jit(solution)/shard_map/merge_out/ppermute | solution.py:17
  84.4 5.3 %collective-permute-done.15.refs_3_ = bf16[2,1,64,1792]{3,2,1,0:T(8,128)(2,1)S(1)} collective-permute-done((bf16[2,1,64,1792]{3,2,1,0:T(8,128)(2,1)}, bf16[2,1,64,1792]{3,2,1,0:T(8,128)(2,1)S(1)}, u32[]{:S(2)}, u32[]{:S(2)}) %collective-permute-start.15) | collective-permute-done | bytes 458784 | tf_op jit(solution)/shard_map/merge_out/ppermute | solution.py:17
  99.8 5.0 merge_qkv.7
  108.5 5.1 merge_qkv.10
  115.2 19.3 %collective-permute-done.19.r3 = bf16[64,3584]{1,0:T(8,128)(2,1)S(1)} collective-permute-done((bf16[64,3584]{1,0:T(8,128)(2,1)S(1)}, bf16[64,3584]{1,0:T(8,128)(2,1)S(1)}, u32[]{:S(2)}, u32[]{:S(2)}) %collective-permute-start.19) | collective-permute-done | bytes 458784 | tf_op jit(solution)/shard_map/merge_out/ppermute | solution.py:17
  134.7 7.4 %collective-permute-done.18.r1 = bf16[64,3584]{1,0:T(8,128)(2,1)S(1)} collective-permute-done((bf16[64,3584]{1,0:T(8,128)(2,1)S(1)}, bf16[64,3584]{1,0:T(8,128)(2,1)S(1)}, u32[]{:S(2)}, u32[]{:S(2)}) %collective-permute-start.18) | collective-permute-done | bytes 458784 | tf_op jit(solution)/shard_map/merge_out/ppermute | solution.py:17
  151.8 7.9 %collective-permute-start.22 = (bf16[256,3584]{1,0:T(8,128)(2,1)}, bf16[256,3584]{1,0:T(8,128)(2,1)S(1)}, u32[]{:S(2)}, u32[]{:S(2)}) collective-permute-start(bf16[256,3584]{1,0:T(8,128)(2,1)} %bitcast.46), channel_id=1, source_target_pairs={{0,1},{1,0},{2,3},{3,2},{4,5},{5,4},{6,7},{7,6},{8,9},{9,8},{10,11... | collective-permute-start | bytes 5505032 | tf_op jit(solution)/shard_map/merge_out/ppermute | solution.py:17
  160.7 5.2 merge_qkv.8
  165.9 5.3 merge_qkv.11
  175.6 8.4 %all-to-all-start = ((bf16[8,16,3584]{2,1,0:T(8,128)(2,1)}), bf16[8,16,3584]{2,1,0:T(8,128)(2,1)}, u32[]{:S(2)}, u32[]{:S(2)}) async-start(bf16[8,16,3584]{2,1,0:T(8,128)(2,1)} %layer.16), calls=%async_computation | async-start | bytes 1835008 | tf_op jit(solution)/shard_map/layer/all_to_all | solution.py:386
  184.0 11.6 %collective-permute-done.5.refs_4_ = bf16[896,512]{1,0:T(8,128)(2,1)} collective-permute-done((bf16[896,512]{1,0:T(8,128)(2,1)S(1)}, bf16[896,512]{1,0:T(8,128)(2,1)}, u32[]{:S(2)}, u32[]{:S(2)}) %collective-permute-start.5) | collective-permute-done | bytes 917536 | tf_op jit(solution)/shard_map/merge_qkv/ppermute | solution.py:17
  200.7 10.0 %collective-permute-done.7.refs_3_ = bf16[384,512]{1,0:T(8,128)(2,1)} collective-permute-done((bf16[384,512]{1,0:T(8,128)(2,1)}, bf16[384,512]{1,0:T(8,128)(2,1)}, u32[]{:S(2)}, u32[]{:S(2)}) %collective-permute-start.7) | collective-permute-done | bytes 393248 | tf_op jit(solution)/shard_map/merge_qkv/ppermute | solution.py:17
  215.0 5.4 %layer.17 = (bf16[128,256]{1,0:T(8,128)(2,1)}, bf16[128,256]{1,0:T(8,128)(2,1)}, bf16[128,512]{1,0:T(8,128)(2,1)}) custom-call(s32[3]{0:T(128)} %pad_add_fusion.idx_ref, bf16[8,16,3584]{2,1,0:T(8,128)(2,1)} %all-to-all-done.x_ref, f32[128,128]{1,0:T(8,128)} %get-tuple-element.31.cos_ref, f32[128,128]{1,0:T(8,128)} %get-tuple-element.30.sin_ref, ...), custom_call_target="tpu_custom_call" | custom-call | tf_op jit(solution)/shard_map/layer/pallas_call | solution.py:154
  222.6 4.4 layer.18
  227.0 33.4 %all_to_all.46.p_ref = bf16[8,16,3584]{2,1,0:T(8,128)(2,1)} all-to-all(bf16[8,16,3584]{2,1,0:T(8,128)(2,1)} %layer.18), channel_id=1, replica_groups={{0,2,4,6,8,10,12,14},{1,3,5,7,9,11,13,15},{16,18,20,22,24,26,28,30},{17..., dimensions={0} | all-to-all | bytes 1835008 | tf_op jit(solution)/shard_map/layer/all_to_all | solution.py:386
  270.6 27.3 %all_to_all.47.x_ref = bf16[8,16,3584]{2,1,0:T(8,128)(2,1)} all-to-all(bf16[8,16,3584]{2,1,0:T(8,128)(2,1)} %layer.20), channel_id=1, replica_groups={{0,2,4,6,8,10,12,14},{1,3,5,7,9,11,13,15},{16,18,20,22,24,26,28,30},{17..., dimensions={0} | all-to-all | bytes 1835008 | tf_op jit(solution)/shard_map/layer/all_to_all | solution.py:386
  297.9 5.4 %layer.21 = (bf16[128,256]{1,0:T(8,128)(2,1)}, bf16[128,256]{1,0:T(8,128)(2,1)}, bf16[128,512]{1,0:T(8,128)(2,1)}) custom-call(s32[3]{0:T(128)} %pad_add_fusion.idx_ref, bf16[8,16,3584]{2,1,0:T(8,128)(2,1)} %all_to_all.47.x_ref, f32[128,128]{1,0:T(8,128)} %get-tuple-element.31.cos_ref, f32[128,128]{1,0:T(8,128)} %get-tuple-element.30.sin_ref, ...), custom_call_target="tpu_custom_call" | custom-call | tf_op jit(solution)/shard_map/layer/pallas_call | solution.py:154
  308.9 4.4 layer.22
  313.3 30.6 %all_to_all.48.p_ref = bf16[8,16,3584]{2,1,0:T(8,128)(2,1)} all-to-all(bf16[8,16,3584]{2,1,0:T(8,128)(2,1)} %layer.22), channel_id=1, replica_groups={{0,2,4,6,8,10,12,14},{1,3,5,7,9,11,13,15},{16,18,20,22,24,26,28,30},{17..., dimensions={0} | all-to-all | bytes 1835008 | tf_op jit(solution)/shard_map/layer/all_to_all | solution.py:386
  354.7 28.9 %all_to_all.49.x_ref = bf16[8,16,3584]{2,1,0:T(8,128)(2,1)} all-to-all(bf16[8,16,3584]{2,1,0:T(8,128)(2,1)} %layer.24), channel_id=1, replica_groups={{0,2,4,6,8,10,12,14},{1,3,5,7,9,11,13,15},{16,18,20,22,24,26,28,30},{17..., dimensions={0} | all-to-all | bytes 1835008 | tf_op jit(solution)/shard_map/layer/all_to_all | solution.py:386
  383.5 5.4 %layer.25 = (bf16[128,256]{1,0:T(8,128)(2,1)}, bf16[128,256]{1,0:T(8,128)(2,1)}, bf16[128,512]{1,0:T(8,128)(2,1)}) custom-call(s32[3]{0:T(128)} %pad_add_fusion.idx_ref, bf16[8,16,3584]{2,1,0:T(8,128)(2,1)} %all_to_all.49.x_ref, f32[128,128]{1,0:T(8,128)} %get-tuple-element.31.cos_ref, f32[128,128]{1,0:T(8,128)} %get-tuple-element.30.sin_ref, ...), custom_call_target="tpu_custom_call" | custom-call | tf_op jit(solution)/shard_map/layer/pallas_call | solution.py:154
  393.0 4.4 layer.26
  397.4 30.6 %all_to_all.50.p_ref = bf16[8,16,3584]{2,1,0:T(8,128)(2,1)} all-to-all(bf16[8,16,3584]{2,1,0:T(8,128)(2,1)} %layer.26), channel_id=1, replica_groups={{0,2,4,6,8,10,12,14},{1,3,5,7,9,11,13,15},{16,18,20,22,24,26,28,30},{17..., dimensions={0} | all-to-all | bytes 1835008 | tf_op jit(solution)/shard_map/layer/all_to_all | solution.py:386
  430.2 4.0 collective-permute-start.27
  439.2 28.9 %all_to_all.51.x_ref = bf16[8,16,3584]{2,1,0:T(8,128)(2,1)} all-to-all(bf16[8,16,3584]{2,1,0:T(8,128)(2,1)} %layer.28), channel_id=1, replica_groups={{0,2,4,6,8,10,12,14},{1,3,5,7,9,11,13,15},{16,18,20,22,24,26,28,30},{17..., dimensions={0} | all-to-all | bytes 1835008 | tf_op jit(solution)/shard_map/layer/all_to_all | solution.py:386
  468.0 5.4 %layer.29 = (bf16[128,256]{1,0:T(8,128)(2,1)}, bf16[128,256]{1,0:T(8,128)(2,1)}, bf16[128,512]{1,0:T(8,128)(2,1)}) custom-call(s32[3]{0:T(128)} %pad_add_fusion.idx_ref, bf16[8,16,3584]{2,1,0:T(8,128)(2,1)} %all_to_all.51.x_ref, f32[128,128]{1,0:T(8,128)} %get-tuple-element.31.cos_ref, f32[128,128]{1,0:T(8,128)} %get-tuple-element.30.sin_ref, ...), custom_call_target="tpu_custom_call" | custom-call | tf_op jit(solution)/shard_map/layer/pallas_call | solution.py:154
  477.5 4.5 layer.30
  485.7 24.0 %all-to-all-done.7.p_ref = bf16[8,16,3584]{2,1,0:T(8,128)(2,1)S(1)} async-done(((bf16[8,16,3584]{2,1,0:T(8,128)(2,1)}), bf16[8,16,3584]{2,1,0:T(8,128)(2,1)S(1)}, u32[]{:S(2)}, u32[]{:S(2)}) %all-to-all-start.7) | async-done | bytes 917536 | tf_op jit(solution)/shard_map/layer/all_to_all | solution.py:386
  515.4 6.1 %all-to-all-start.8 = ((f32[16,1,1]{2,1,0:T(1,128)}), f32[16,1,1]{2,1,0:T(1,128)S(1)}, u32[]{:S(2)}, u32[]{:S(2)}) async-start(f32[16,1,1]{2,1,0:T(1,128)} %broadcast_in_dim.29), calls=%async_computation.8 | async-start | bytes 16384 | tf_op jit(solution)/shard_map/loss/all_to_all | solution.py:421
  521.5 7.1 %all-to-all-done.8 = f32[16,1,1]{2,1,0:T(1,128)S(1)} async-done(((f32[16,1,1]{2,1,0:T(1,128)}), f32[16,1,1]{2,1,0:T(1,128)S(1)}, u32[]{:S(2)}, u32[]{:S(2)}) %all-to-all-start.8) | async-done | bytes 96 | tf_op jit(solution)/shard_map/loss/all_to_all | solution.py:421
  (151 shorter events, 121.3 us)
Async XLA Ops:
  9.6 89.0 %collective-permute-start = (bf16[2,2,896,256]{3,2,1,0:T(8,128)(2,1)}, bf16[2,2,896,256]{3,2,1,0:T(8,128)(2,1)S(1)}, u32[]{:S(2)}, u32[]{:S(2)}) collective-permute-start(bf16[2,2,896,256]{3,2,1,0:T(8,128)(2,1)} %merge_qkv.6), channel_id=1, source_target_pairs={{0,16},{16,0},{32,48},{48,32},{1,17},{17,1},{33,49},{49,33},{2,18}... | collective-permute-start | bytes 5505032 | tf_op jit(solution)/shard_map/merge_qkv/ppermute | solution.py:17
  18.5 88.7 %collective-permute-start.2 = (bf16[2,2,896,256]{3,2,1,0:T(8,128)(2,1)}, bf16[2,2,896,256]{3,2,1,0:T(8,128)(2,1)S(1)}, u32[]{:S(2)}, u32[]{:S(2)}) collective-permute-start(bf16[2,2,896,256]{3,2,1,0:T(8,128)(2,1)} %merge_qkv.9), channel_id=1, source_target_pairs={{0,48},{16,32},{32,16},{48,0},{1,49},{17,33},{33,17},{49,1},{2,50}... | collective-permute-start | bytes 5505032 | tf_op jit(solution)/shard_map/merge_qkv/ppermute | solution.py:17
  23.8 46.2 %collective-permute-start.14 = (bf16[2,2,64,1792]{3,2,1,0:T(8,128)(2,1)}, bf16[2,2,64,1792]{3,2,1,0:T(8,128)(2,1)S(1)}, u32[]{:S(2)}, u32[]{:S(2)}) collective-permute-start(bf16[2,2,64,1792]{3,2,1,0:T(8,128)(2,1)} %merge_out.7), channel_id=1, source_target_pairs={{0,16},{16,0},{32,48},{48,32},{1,17},{17,1},{33,49},{49,33},{2,18}... | collective-permute-start | bytes 2752520 | tf_op jit(solution)/shard_map/merge_out/ppermute | solution.py:17
  27.6 52.3 %collective-permute-start.16 = (bf16[2,2,64,1792]{3,2,1,0:T(8,128)(2,1)}, bf16[2,2,64,1792]{3,2,1,0:T(8,128)(2,1)S(1)}, u32[]{:S(2)}, u32[]{:S(2)}) collective-permute-start(bf16[2,2,64,1792]{3,2,1,0:T(8,128)(2,1)} %merge_out.10), channel_id=1, source_target_pairs={{0,48},{16,32},{32,16},{48,0},{1,49},{17,33},{33,17},{49,1},{2,50}... | collective-permute-start | bytes 2752520 | tf_op jit(solution)/shard_map/merge_out/ppermute | solution.py:17
  74.4 15.3 %collective-permute-start.15 = (bf16[2,1,64,1792]{3,2,1,0:T(8,128)(2,1)}, bf16[2,1,64,1792]{3,2,1,0:T(8,128)(2,1)S(1)}, u32[]{:S(2)}, u32[]{:S(2)}) collective-permute-start(bf16[2,1,64,1792]{3,2,1,0:T(8,128)(2,1)} %merge_out.8), channel_id=1, source_target_pairs={{0,48},{16,32},{32,16},{48,0},{1,49},{17,33},{33,17},{49,1},{2,50}... | collective-permute-start | bytes 1376264 | tf_op jit(solution)/shard_map/merge_out/ppermute | solution.py:17
  84.4 9.8 %collective-permute-start.17 = (bf16[2,1,64,1792]{3,2,1,0:T(8,128)(2,1)}, bf16[2,1,64,1792]{3,2,1,0:T(8,128)(2,1)S(1)}, u32[]{:S(2)}, u32[]{:S(2)}) collective-permute-start(bf16[2,1,64,1792]{3,2,1,0:T(8,128)(2,1)} %merge_out.11), channel_id=1, source_target_pairs={{0,16},{16,0},{32,48},{48,32},{1,17},{17,1},{33,49},{49,33},{2,18}... | collective-permute-start | bytes 1376264 | tf_op jit(solution)/shard_map/merge_out/ppermute | solution.py:17
  104.9 54.9 %collective-permute-start.1 = (bf16[2,1,896,256]{3,2,1,0:T(8,128)(2,1)}, bf16[2,1,896,256]{3,2,1,0:T(8,128)(2,1)S(1)}, u32[]{:S(2)}, u32[]{:S(2)}) collective-permute-start(bf16[2,1,896,256]{3,2,1,0:T(8,128)(2,1)} %merge_qkv.7), channel_id=1, source_target_pairs={{0,48},{16,32},{32,16},{48,0},{1,49},{17,33},{33,17},{49,1},{2,50}... | collective-permute-start | bytes 2752520 | tf_op jit(solution)/shard_map/merge_qkv/ppermute | solution.py:17
  113.5 52.3 %collective-permute-start.3 = (bf16[2,1,896,256]{3,2,1,0:T(8,128)(2,1)}, bf16[2,1,896,256]{3,2,1,0:T(8,128)(2,1)}, u32[]{:S(2)}, u32[]{:S(2)}) collective-permute-start(bf16[2,1,896,256]{3,2,1,0:T(8,128)(2,1)} %merge_qkv.10), channel_id=1, source_target_pairs={{0,16},{16,0},{32,48},{48,32},{1,17},{17,1},{33,49},{49,33},{2,18}... | collective-permute-start | bytes 2752520 | tf_op jit(solution)/shard_map/merge_qkv/ppermute | solution.py:17
  113.6 21.0 %collective-permute-start.19 = (bf16[64,3584]{1,0:T(8,128)(2,1)S(1)}, bf16[64,3584]{1,0:T(8,128)(2,1)S(1)}, u32[]{:S(2)}, u32[]{:S(2)}) collective-permute-start(bf16[64,3584]{1,0:T(8,128)(2,1)S(1)} %pad_maximum_fusion.1.r0), channel_id=1, source_target_pairs={{0,48},{16,32},{32,16},{48,0},{1,49},{17,33},{33,17},{49,1},{2,50}... | collective-permute-start | bytes 1376264 | tf_op jit(solution)/shard_map/merge_out/ppermute | solution.py:17
  114.0 28.1 %collective-permute-start.18 = (bf16[64,3584]{1,0:T(8,128)(2,1)S(1)}, bf16[64,3584]{1,0:T(8,128)(2,1)S(1)}, u32[]{:S(2)}, u32[]{:S(2)}) collective-permute-start(bf16[64,3584]{1,0:T(8,128)(2,1)S(1)} %pad_maximum_fusion.1.r0), channel_id=1, source_target_pairs={{0,16},{16,0},{32,48},{48,32},{1,17},{17,1},{33,49},{49,33},{2,18}... | collective-permute-start | bytes 1376264 | tf_op jit(solution)/shard_map/merge_out/ppermute | solution.py:17
  134.6 12.4 %collective-permute-start.20 = (bf16[64,1792]{1,0:T(8,128)(2,1)S(1)}, bf16[64,1792]{1,0:T(8,128)(2,1)S(1)}, u32[]{:S(2)}, u32[]{:S(2)}) collective-permute-start(bf16[64,1792]{1,0:T(8,128)(2,1)S(1)} %slice.26), channel_id=1, source_target_pairs={{0,16},{16,0},{32,48},{48,32},{1,17},{17,1},{33,49},{49,33},{2,18}... | collective-permute-start | bytes 688136 | tf_op jit(solution)/shard_map/merge_out/ppermute | solution.py:17
  142.1 6.2 %collective-permute-start.21 = (bf16[64,1792]{1,0:T(8,128)(2,1)S(1)}, bf16[64,1792]{1,0:T(8,128)(2,1)S(1)}, u32[]{:S(2)}, u32[]{:S(2)}) collective-permute-start(bf16[64,1792]{1,0:T(8,128)(2,1)S(1)} %slice.27), channel_id=1, source_target_pairs={{0,48},{16,32},{32,16},{48,0},{1,49},{17,33},{33,17},{49,1},{2,50}... | collective-permute-start | bytes 688136 | tf_op jit(solution)/shard_map/merge_out/ppermute | solution.py:17
  151.8 68.9 %collective-permute-start.22 = (bf16[256,3584]{1,0:T(8,128)(2,1)}, bf16[256,3584]{1,0:T(8,128)(2,1)S(1)}, u32[]{:S(2)}, u32[]{:S(2)}) collective-permute-start(bf16[256,3584]{1,0:T(8,128)(2,1)} %bitcast.46), channel_id=1, source_target_pairs={{0,1},{1,0},{2,3},{3,2},{4,5},{5,4},{6,7},{7,6},{8,9},{9,8},{10,11... | collective-permute-start | bytes 5505032 | tf_op jit(solution)/shard_map/merge_out/ppermute | solution.py:17
  172.3 23.4 %collective-permute-start.5 = (bf16[896,512]{1,0:T(8,128)(2,1)S(1)}, bf16[896,512]{1,0:T(8,128)(2,1)}, u32[]{:S(2)}, u32[]{:S(2)}) collective-permute-start(bf16[896,512]{1,0:T(8,128)(2,1)S(1)} %pad_maximum_fusion.refs_0_), channel_id=1, source_target_pairs={{0,48},{16,32},{32,16},{48,0},{1,49},{17,33},{33,17},{49,1},{2,50}... | collective-permute-start | bytes 2752520 | tf_op jit(solution)/shard_map/merge_qkv/ppermute | solution.py:17
  172.6 24.9 %collective-permute-start.4 = (bf16[896,512]{1,0:T(8,128)(2,1)S(1)}, bf16[896,512]{1,0:T(8,128)(2,1)}, u32[]{:S(2)}, u32[]{:S(2)}) collective-permute-start(bf16[896,512]{1,0:T(8,128)(2,1)S(1)} %pad_maximum_fusion.refs_0_), channel_id=1, source_target_pairs={{0,16},{16,0},{32,48},{48,32},{1,17},{17,1},{33,49},{49,33},{2,18}... | collective-permute-start | bytes 2752520 | tf_op jit(solution)/shard_map/merge_qkv/ppermute | solution.py:17
  172.7 28.0 %collective-permute-start.8 = (bf16[896,512]{1,0:T(8,128)(2,1)S(1)}, bf16[896,512]{1,0:T(8,128)(2,1)}, u32[]{:S(2)}, u32[]{:S(2)}) collective-permute-start(bf16[896,512]{1,0:T(8,128)(2,1)S(1)} %pad_maximum_fusion.refs_0_), channel_id=1, source_target_pairs={{0,1},{1,0},{2,3},{3,2},{4,5},{5,4},{6,7},{7,6},{8,9},{9,8},{10,11... | collective-permute-start | bytes 2752520 | tf_op jit(solution)/shard_map/merge_qkv/ppermute | solution.py:17
  175.6 38.0 %all-to-all-start = ((bf16[8,16,3584]{2,1,0:T(8,128)(2,1)}), bf16[8,16,3584]{2,1,0:T(8,128)(2,1)}, u32[]{:S(2)}, u32[]{:S(2)}) async-start(bf16[8,16,3584]{2,1,0:T(8,128)(2,1)} %layer.16), calls=%async_computation | async-start | bytes 1835008 | tf_op jit(solution)/shard_map/layer/all_to_all | solution.py:386
  197.5 14.8 %collective-permute-start.6 = (bf16[512,512]{1,0:T(8,128)(2,1)}, bf16[512,512]{1,0:T(8,128)(2,1)S(1)}, u32[]{:S(2)}, u32[]{:S(2)}) collective-permute-start(bf16[512,512]{1,0:T(8,128)(2,1)} %slice.24), channel_id=1, source_target_pairs={{0,16},{16,0},{32,48},{48,32},{1,17},{17,1},{33,49},{49,33},{2,18}... | collective-permute-start | bytes 1572872 | tf_op jit(solution)/shard_map/merge_qkv/ppermute | solution.py:17
  199.3 11.4 %collective-permute-start.7 = (bf16[384,512]{1,0:T(8,128)(2,1)}, bf16[384,512]{1,0:T(8,128)(2,1)}, u32[]{:S(2)}, u32[]{:S(2)}) collective-permute-start(bf16[384,512]{1,0:T(8,128)(2,1)} %slice.25), channel_id=1, source_target_pairs={{0,48},{16,32},{32,16},{48,0},{1,49},{17,33},{33,17},{49,1},{2,50}... | collective-permute-start | bytes 1179656 | tf_op jit(solution)/shard_map/merge_qkv/ppermute | solution.py:17
  199.6 14.5 %collective-permute-start.12 = (bf16[896,512]{1,0:T(8,128)(2,1)}, bf16[896,512]{1,0:T(8,128)(2,1)}, u32[]{:S(2)}, u32[]{:S(2)}) collective-permute-start(bf16[896,512]{1,0:T(8,128)(2,1)} %collective-permute-done.5.refs_4_), channel_id=1, source_target_pairs={{0,1},{1,0},{2,3},{3,2},{4,5},{5,4},{6,7},{7,6},{8,9},{9,8},{10,11... | collective-permute-start | bytes 2752520 | tf_op jit(solution)/shard_map/merge_qkv/ppermute | solution.py:17
  200.7 13.4 %collective-permute-start.9 = (bf16[896,512]{1,0:T(8,128)(2,1)}, bf16[896,512]{1,0:T(8,128)(2,1)S(1)}, u32[]{:S(2)}, u32[]{:S(2)}) collective-permute-start(bf16[896,512]{1,0:T(8,128)(2,1)} %collective-permute-done.4.refs_1_), channel_id=1, source_target_pairs={{0,1},{1,0},{2,3},{3,2},{4,5},{5,4},{6,7},{7,6},{8,9},{9,8},{10,11... | collective-permute-start | bytes 2752520 | tf_op jit(solution)/shard_map/merge_qkv/ppermute | solution.py:17
  210.7 3.4 collective-permute-start.11
  212.4 2.2 collective-permute-start.10
  220.4 1.6 collective-permute-start.13
  262.6 5.3 collective-permute-start.23
  303.2 5.0 collective-permute-start.24
  346.0 6.0 %collective-permute-start.25 = (bf16[16,3584]{1,0:T(8,128)(2,1)}, bf16[16,3584]{1,0:T(8,128)(2,1)S(1)}, u32[]{:S(2)}, u32[]{:S(2)}) collective-permute-start(bf16[16,3584]{1,0:T(8,128)(2,1)} %layer.23), channel_id=1, source_target_pairs={{0,64},{64,128},{128,192},{1,65},{65,129},{129,193},{2,66},{66,130... | collective-permute-start | bytes 344072 | tf_op jit(solution)/shard_map/layer/ppermute | solution.py:403
  388.9 3.4 collective-permute-start.26
  430.2 6.3 %collective-permute-start.27 = (bf16[16,3584]{1,0:T(8,128)(2,1)}, bf16[16,3584]{1,0:T(8,128)(2,1)S(1)}, u32[]{:S(2)}, u32[]{:S(2)}) collective-permute-start(bf16[16,3584]{1,0:T(8,128)(2,1)} %layer.27), channel_id=1, source_target_pairs={{0,64},{64,128},{128,192},{1,65},{65,129},{129,193},{2,66},{66,130... | collective-permute-start | bytes 344072 | tf_op jit(solution)/shard_map/layer/ppermute | solution.py:403
  473.4 3.4 collective-permute-start.28
  482.0 27.7 %all-to-all-start.7 = ((bf16[8,16,3584]{2,1,0:T(8,128)(2,1)}), bf16[8,16,3584]{2,1,0:T(8,128)(2,1)S(1)}, u32[]{:S(2)}, u32[]{:S(2)}) async-start(bf16[8,16,3584]{2,1,0:T(8,128)(2,1)} %layer.30), calls=%async_computation.7 | async-start | bytes 1835008 | tf_op jit(solution)/shard_map/layer/all_to_all | solution.py:386
  515.4 13.1 %all-to-all-start.8 = ((f32[16,1,1]{2,1,0:T(1,128)}), f32[16,1,1]{2,1,0:T(1,128)S(1)}, u32[]{:S(2)}, u32[]{:S(2)}) async-start(f32[16,1,1]{2,1,0:T(1,128)} %broadcast_in_dim.29), calls=%async_computation.8 | async-start | bytes 16384 | tf_op jit(solution)/shard_map/loss/all_to_all | solution.py:421
  (32 other events, 246.5 us)

commit v2 on v1

v2 whole, which is shorter than its diff:
```python
import functools

import jax
import jax.numpy as jnp
from jax import lax
from jax.experimental import pallas as pl
from jax.experimental.pallas import tpu as pltpu
from jax.sharding import PartitionSpec as P

HEAD_DIM = 256
F32 = jnp.float32
BF16 = jnp.bfloat16
SMEM = pltpu.SMEM
VMEM = pltpu.VMEM
HBM = pltpu.HBM


def exchanged(array, axis, mask):
    return lax.ppermute(array, axis, [(i, i ^ mask) for i in range(lax.axis_size(axis))])


def placed(array, space):
    return pltpu.with_memory_space_constraint(array, space)


def result_on_chip(shape, dtype=BF16):
    return VMEM(shape, dtype)


def kernel_call(kernel, operands, spaces, shapes, scratch=(), mib=16):
    operands = [a if space == SMEM else placed(a, space) for a, space in zip(operands, spaces)]
    outs = pl.pallas_call(
        kernel,
        out_shape=tuple(result_on_chip(shape) for shape in shapes),
        in_specs=[pl.BlockSpec(memory_space=space) for space in spaces],
        out_specs=tuple(pl.BlockSpec(memory_space=VMEM) for _ in shapes),
        scratch_shapes=scratch,
        compiler_params=pltpu.CompilerParams(vmem_limit_bytes=mib * 1024 * 1024),
    )(*operands)
    return outs[0] if len(shapes) == 1 else outs


def share_call(plan, scale, source, base, count, received, finish):
    weights, fishers, rows, widths, cut = source
    n = len(weights)
    sub = rows // 2
    parts = count * 2
    strip = 64 if sub % 64 == 0 and sub > 64 else 16
    total = sum(widths)
    entries = [entry for _, entry in received]

    def kernel(plan_ref, scale_ref, *refs):
        arrays = refs[: 2 * n]
        gots = refs[2 * n : 2 * n + len(entries)]
        out_ref = refs[2 * n + len(entries)]
        buffers = refs[2 * n + len(entries) + 1 : -1]
        sems = refs[-1]

        def copy(k, part):
            return pltpu.make_async_copy(
                cut(arrays[k], plan_ref[base + part // 2], (part % 2) * sub, sub),
                buffers[k].at[part],
                sems.at[k, part],
            )

        for part in range(parts):
            for k in range(2 * n):
                copy(k, part).start()
        task_scale = scale_ref[0]
        got_blocks = [0 if entry is None else plan_ref[entry] for entry in entries]

        def strip_of(part, i):
            inside = pl.ds(pl.multiple_of(i * strip, strip), strip)
            lines = pl.ds(pl.multiple_of((part % 2) * sub + i * strip, strip), strip)
            at = 0
            for k in range(n):
                scaled = buffers[n + k][part, inside, :].astype(F32) * task_scale
                term = scaled * buffers[k][part, inside, :].astype(F32)
                sums = [term.astype(BF16), scaled.astype(BF16)]
                cols = slice(at, at + widths[k])
                at += widths[k]
                for got, block in zip(gots, got_blocks):
                    sums = [
                        v.astype(F32) + got[i, block, lines, cols].astype(F32)
                        for i, v in enumerate(sums)
                    ]
                if finish:
                    out_ref[lines, cols] = (sums[0] / sums[1]).astype(BF16)
                else:
                    out_ref[0, part // 2, lines, cols] = sums[0].astype(BF16)
                    out_ref[1, part // 2, lines, cols] = sums[1].astype(BF16)

        def one_part(part, carry):
            for k in range(2 * n):
                copy(k, part).wait()
            lax.fori_loop(0, sub // strip, lambda i, c: (strip_of(part, i), c)[1], 0)
            return carry

        lax.fori_loop(0, parts, one_part, 0)

    scratch = [VMEM((parts, sub, widths[k % n]), BF16) for k in range(2 * n)]
    scratch.append(pltpu.SemaphoreType.DMA((2 * n, parts)))
    return kernel_call(
        kernel,
        [plan, scale, *weights, *fishers, *(array for array, _ in received)],
        [SMEM, SMEM] + [HBM] * (2 * n) + [VMEM] * len(entries),
        [(rows, total) if finish else (2, count, rows, total)],
        scratch,
    )


def normed_copies(states, gain, copies):
    rows, width = states.shape

    def kernel(states_ref, gain_ref, out_ref):
        x = states_ref[...].astype(F32)
        scale = lax.rsqrt(jnp.mean(x * x, axis=-1, keepdims=True) + 1e-06)
        y = (x * scale * gain_ref[...]).astype(BF16)
        for k in range(copies):
            out_ref[k] = y

    return kernel_call(kernel, [states, gain], [VMEM] * 2, [(copies, rows, width)])


def project(idx, normed, own, peer, cosine, sine):
    copies, rows, width = normed.shape
    tokens = copies * rows
    quarter = width // 4

    def kernel(idx_ref, x_ref, cos_ref, sin_ref, *refs):
        q_own_ref, q_peer_ref, kv_ref = refs[-3:]
        x_index = idx_ref[0]
        core = idx_ref[1]
        sums = [None] * 4
        for d in range(4):
            at = pl.multiple_of((x_index ^ d) * quarter, 128)
            part = x_ref[:, :, pl.ds(at, quarter)].reshape(tokens, quarter)
            for k in range(4):
                prod = jnp.dot(part, refs[4 * k + d][...], preferred_element_type=F32)
                sums[k] = prod if d == 0 else sums[k] + prod
        q_mine, mine, q_theirs, theirs = sums
        cos = cos_ref[...]
        sin = sin_ref[...]
        for ref, q in ((q_own_ref, q_mine), (q_peer_ref, q_theirs)):
            a = q[:, :128]
            b = q[:, 128:]
            ref[:, :128] = (a * cos - b * sin).astype(BF16)
            ref[:, 128:] = (b * cos + a * sin).astype(BF16)
        first = core == 0
        k_mine = mine[:, :128].astype(BF16).astype(F32)
        k_theirs = theirs[:, :128].astype(BF16).astype(F32)
        a = jnp.where(first, k_mine, k_theirs)
        b = jnp.where(first, k_theirs, k_mine)
        kv_ref[:, :128] = (a * cos - b * sin).astype(BF16)
        kv_ref[:, 128:256] = (b * cos + a * sin).astype(BF16)
        kv_ref[:, 256:384] = jnp.where(first, mine[:, 128:], theirs[:, 128:]).astype(BF16)
        kv_ref[:, 384:] = jnp.where(first, theirs[:, 128:], mine[:, 128:]).astype(BF16)

    return kernel_call(
        kernel,
        [idx, normed, cosine, sine, *own[0], *own[1], *peer[0], *peer[1]],
        [SMEM] + [VMEM] * 19,
        [(tokens, 256), (tokens, 256), (tokens, 512)],
    )


def attend(idx, q_own, q_peer, kv_own, kv_peer, own, peer, copies):
    tokens = q_own.shape[0]
    rows = tokens // copies
    quarter = own[0][0].shape[1]

    def kernel(idx_ref, qo_ref, qp_ref, ko_ref, kp_ref, *refs):
        out_ref = refs[-1]
        x_index = idx_ref[0]
        core = idx_ref[1]
        length = idx_ref[2]

        def positions(shape, dim, which):
            i = lax.broadcasted_iota(jnp.int32, shape, dim)
            return (i // rows) * (2 * rows) + which * rows + i % rows

        shape = (tokens, tokens)
        q_pos = positions(shape, 0, core)
        masks = []
        for which in (core, 1 - core):
            k_pos = positions(shape, 1, which)
            masks.append((k_pos <= q_pos) & (k_pos < length))
        contexts = []
        for q_ref in (qo_ref, qp_ref):
            q = q_ref[...]
            numerators = []
            for kv_ref, allowed in ((ko_ref, masks[0]), (kp_ref, masks[1])):
                scores = lax.dot_general(
                    q,
                    kv_ref[:, :256],
                    (((1,), (1,)), ((), ())),
                    preferred_element_type=F32,
                ) * HEAD_DIM ** (-0.5)
                capped = 50.0 * jnp.tanh(scores / 50.0)
                numerators.append(jnp.where(allowed, jnp.exp(capped), 0.0))
            total = jnp.sum(numerators[0], axis=-1, keepdims=True) + jnp.sum(
                numerators[1], axis=-1, keepdims=True
            )
            ctx = None
            for num, kv_ref in zip(numerators, (ko_ref, kp_ref)):
                prod = jnp.dot(
                    (num / total).astype(BF16), kv_ref[:, 256:], preferred_element_type=F32
                )
                ctx = prod if ctx is None else ctx + prod
            contexts.append(ctx.astype(BF16))
        lefts = [c[:, h * 128 : (h + 1) * 128] for c in contexts for h in range(2)]
        for d in range(4):
            out = None
            for k in range(4):
                prod = jnp.dot(lefts[k], refs[4 * k + d][...], preferred_element_type=F32)
                out = prod if out is None else out + prod
            at = pl.multiple_of((x_index ^ d) * quarter, 128)
            out_ref[:, :, pl.ds(at, quarter)] = out.astype(BF16).reshape(copies, rows, quarter)

    return kernel_call(
        kernel,
        [idx, q_own, q_peer, kv_own, kv_peer, *own[0], *own[1], *peer[0], *peer[1]],
        [SMEM] + [VMEM] * 20,
        [(copies, rows, 4 * quarter)],
    )


def finished(pieces, states, gain):
    def kernel(p_ref, states_ref, gain_ref, out_ref):
        total = jnp.sum(p_ref[...].astype(F32), axis=0)
        scale = lax.rsqrt(jnp.mean(total * total, axis=-1, keepdims=True) + 1e-06)
        out = states_ref[...].astype(F32) + total * scale * gain_ref[...]
        out_ref[...] = out.astype(BF16)

    return kernel_call(kernel, [pieces, states, gain], [VMEM] * 3, [states.shape])


NEAR, FAR = 1, 3


def first_halves(plan, scale, sources):
    sent = [share_call(plan, scale, s, 8 * i, 2, (), False) for i, s in enumerate(sources)]
    return [exchanged(s, "task", (NEAR, FAR)[i]) for i, s in enumerate(sent)]


def second_halves(plan, scale, sources, got):
    sent = [
        share_call(plan, scale, s, 8 * i + 2, 1, ((got[i], 8 * i + 3),), False)
        for i, s in enumerate(sources)
    ]
    return sent, [exchanged(s, "task", (FAR, NEAR)[i]) for i, s in enumerate(sent)]


def shares(plan, scale, sources, got, more):
    return [
        share_call(plan, scale, s, 8 * i + 4, 1, ((got[i], 8 * i + 5), (more[i], None)), True)
        for i, s in enumerate(sources)
    ]


def neighbours(own):
    near = [exchanged(o, "task", NEAR) for o in own]
    far = [exchanged(o, "task", FAR) for o in own]
    return near, far


def completed(own, near, far):
    opposite = [exchanged(far[0], "task", NEAR), exchanged(near[1], "task", FAR)]
    return [(own[i], near[i], opposite[i], far[i]) for i in range(2)]


def gathered(own):
    return completed(own, *neighbours(own))


def of_partner(pieces):
    return [tuple(exchanged(p, "mp", 1) for p in group) for group in pieces]


def per_device(
    hidden_in,
    lengths,
    layer_targets,
    task_weights,
    norm_gains,
    query_weight,
    key_weight,
    value_weight,
    output_weight,
    query_fisher,
    key_fisher,
    value_fisher,
    output_fisher,
):
    x_index = lax.axis_index("task")
    mp_index = lax.axis_index("mp")
    section_index = lax.axis_index("section")
    core = mp_index % 2
    chips = lax.axis_size("mp") // 2
    groups = [[2 * z + c for z in range(chips)] for c in range(2)]
    sections = lax.axis_size("section")
    states = hidden_in[0]
    rows, width = states.shape
    length = lengths[0]
    pre_gain = norm_gains[0, 0:1]
    post_gain = norm_gains[0, 1:2]
    scale = lax.dynamic_slice_in_dim(task_weights, x_index, 1)

    b = x_index // 2
    a = (x_index % 2) ^ b

    def block_a(h1, h2):
        return jnp.where(h1 == 0, 3 * h2, 1 + h2)

    def block_b(h1, h2):
        return jnp.where(h1 == 0, h2, 3 - h2)

    zero = jnp.zeros_like(a)
    plan = jnp.stack(
        [
            block_a(1 - a, 0),
            block_a(1 - a, 1),
            block_a(a, 1 - b),
            1 - b,
            x_index,
            b,
            zero,
            zero,
            block_b(1 - b, 0),
            block_b(1 - b, 1),
            block_b(b, 1 - a),
            1 - a,
            x_index,
            a,
            zero,
            zero,
        ]
    ).astype(jnp.int32)
    scalars = jnp.stack([x_index, core, length]).astype(jnp.int32)

    def quarters(array):
        array = array[0, 0]
        return array.reshape(4, array.shape[0] // 4, array.shape[1])

    def cut_rows(ref, block, row, sub):
        return ref.at[block, pl.ds(row, sub), :]

    def cut_columns(start):
        def cut(ref, block, row, sub):
            at = pl.multiple_of(block * (width // 4), 128)
            return ref.at[pl.ds(start + row, sub), pl.ds(at, width // 4)]

        return cut

    qkv_sources = (
        ((quarters(query_weight),), (quarters(query_fisher),), width // 4, (256,), cut_rows),
        (
            (quarters(key_weight), quarters(value_weight)),
            (quarters(key_fisher), quarters(value_fisher)),
            width // 4,
            (128, 128),
            cut_rows,
        ),
    )
    out_sources = tuple(
        (
            (output_weight[0, 0],),
            (output_fisher[0, 0],),
            128,
            (width // 4,),
            cut_columns(start),
        )
        for start in (0, 128)
    )

    positions = (
        2 * rows * jnp.arange(chips, dtype=jnp.int32)[:, None]
        + core * rows
        + jnp.arange(rows, dtype=jnp.int32)[None, :]
    ).reshape(-1)
    frequency = 10000.0 ** (-2.0 * jnp.arange(HEAD_DIM // 2, dtype=F32) / HEAD_DIM)
    angles = positions.astype(F32)[:, None] * frequency[None, :]
    cosine = jnp.cos(angles)
    sine = jnp.sin(angles)

    def spread(array):
        return lax.all_to_all(array, "mp", 0, 0, tiled=True, axis_index_groups=groups)

    def projected(normed):
        q_own, q_peer, kv_own = project(scalars, normed, qkv_own, qkv_peer, cosine, sine)
        return q_own, q_peer, kv_own, exchanged(kv_own, "mp", 1)

    with jax.named_scope("merge"):
        qkv_got = first_halves(plan, scale, qkv_sources)
        first_normed = spread(normed_copies(states, pre_gain, chips))
        out_got = first_halves(plan, scale, out_sources)
        qkv_got, first_normed, cosine, sine = lax.optimization_barrier(
            (qkv_got, first_normed, cosine, sine)
        )
        qkv_sent, qkv_more = second_halves(plan, scale, qkv_sources, qkv_got)
        out_got, _ = lax.optimization_barrier((out_got, qkv_sent))
        out_sent, out_more = second_halves(plan, scale, out_sources, out_got)
        qkv_share = shares(plan, scale, qkv_sources, qkv_got, qkv_more)
        out_more, _ = lax.optimization_barrier((out_more, qkv_share))
        out_share = shares(plan, scale, out_sources, out_got, out_more)
        qkv_own = gathered(qkv_share)
        qkv_peer = of_partner(qkv_own)
        out_first = neighbours(out_share)
    with jax.named_scope("layer"):
        queries = projected(first_normed)
    with jax.named_scope("merge"):
        out_first, _ = lax.optimization_barrier((out_first, queries[0]))
        out_own = completed(out_share, *out_first)
        out_peer = of_partner(out_own)

    chosen = None
    for step in range(sections):
        with jax.named_scope("layer"):
            if step > 0:
                states = lax.ppermute(
                    layer_out, "section", [(i, i + 1) for i in range(sections - 1)]
                )
                queries = projected(spread(normed_copies(states, pre_gain, chips)))
            partial = attend(scalars, *queries, out_own, out_peer, chips)
            layer_out = finished(spread(partial), states, post_gain)
            chosen = (
                layer_out
                if chosen is None
                else jnp.where(section_index == step, layer_out, chosen)
            )
    with jax.named_scope("loss"):
        own_positions = mp_index * rows + jnp.arange(rows, dtype=jnp.int32)
        mismatch = chosen.astype(F32) - layer_targets[0, 0].astype(F32)
        loss_part = jnp.sum(jnp.where((own_positions < length)[:, None], mismatch * mismatch, 0.0))
        copies = jnp.broadcast_to(loss_part, (2 * chips, 1))
        total = jnp.sum(lax.all_to_all(copies, "mp", 0, 0, tiled=True))
        loss = total / (length.astype(F32) * width)
    return (chosen[None, None], loss[None, None])


def solution(mesh):
    in_specs = (
        P("task", "mp", None),
        P("task"),
        P("section", "task", "mp", None),
        P(),
        P("section", None, None),
        P("task", "section", None, "mp"),
        P("task", "section", None, "mp"),
        P("task", "section", None, "mp"),
        P("task", "section", "mp", None),
        P("task", "section", None, "mp"),
        P("task", "section", None, "mp"),
        P("task", "section", None, "mp"),
        P("task", "section", "mp", None),
    )
    out_specs = (P("section", "task", "mp", None), P("section", "task"))
    return jax.shard_map(
        per_device, mesh=mesh, in_specs=in_specs, out_specs=out_specs, check_vma=False
    )
```

time: 534 us -> 444 us (0.83)
  Pallas kernels: 114 us -> 60.1 us
  waiting for transfers between devices: 146 us -> 113 us
  starting transfers between devices: 62 us -> 82.8 us
  local copies, waits for them, and re-layouts: 21.2 us -> 3.6 us
  blocking collectives: 180 us -> 173 us
    pallas_call x29 -> x28, Pallas kernels: 114 us -> 60.1 us  [kernel_call(): pl.pallas_call(kernel, out_shape=tuple((result_on_chip(shape) for shape i...]
    ppermute x26 -> x40, waiting for transfers between devices: 108 us -> 59.3 us  [exchanged(): lax.ppermute(array, axis, [(i, i ^ mask) for i in range(lax.axis_size(axi...]
    ppermute x26 -> x40, starting transfers between devices: 33 us -> 53.5 us  [exchanged(): lax.ppermute(array, axis, [(i, i ^ mask) for i in range(lax.axis_size(axi...]
    all_to_all x2, waiting for transfers between devices: 24 us -> 41.2 us  [spread(): lax.all_to_all(array, 'mp', 0, 0, tiled=True, axis_index_groups=groups)]
    unnamed x64 -> x8, local copies, waits for them, and re-layouts: 13.6 us -> 0.95 us
    all_to_all x6, blocking collectives: 180 us -> 173 us  [spread(): lax.all_to_all(array, 'mp', 0, 0, tiled=True, axis_index_groups=groups)]
  transfers between devices with their start and end apart: 32 -> 46, of which waited for: 20 -> 22; matrix products, arithmetic and copies ran while one was open for 1% -> 0% of each run, Pallas kernels for 11% -> 9%
where the time goes in v2:
time: 444 us; the launch traced here: 439 us
  blocking collectives  173 us (39%)
  waiting for transfers between devices  113 us (25%)
  starting transfers between devices  82.8 us (19%)
  Pallas kernels  60.1 us (14%)
    all_to_all x6, blocking collectives, spread(): lax.all_to_all(array, 'mp', 0, 0, tiled=True, axis_index_groups=groups)  173 us
    pallas_call x28, Pallas kernels, kernel_call(): pl.pallas_call(kernel, out_shape=tuple((result_on_chip(shape) for shape i...  60.1 us
    ppermute x40, waiting for transfers between devices, exchanged(): lax.ppermute(array, axis, [(i, i ^ mask) for i in range(lax.axis_size(axi...  59.3 us
    ppermute x40, starting transfers between devices, exchanged(): lax.ppermute(array, axis, [(i, i ^ mask) for i in range(lax.axis_size(axi...  53.5 us
    all_to_all x2, waiting for transfers between devices, spread(): lax.all_to_all(array, 'mp', 0, 0, tiled=True, axis_index_groups=groups)  41.2 us
    all_to_all x2, starting transfers between devices, spread(): lax.all_to_all(array, 'mp', 0, 0, tiled=True, axis_index_groups=groups)  11.9 us
    ppermute x3, starting transfers between devices, per_device(): lax.ppermute(layer_out, 'section', [(i, i + 1) for i in range(sections -...  11.4 us
  transfers between devices with their start and end apart: 46, of which 22 were waited for; matrix products, arithmetic and copies ran while one was open for 0% of the time, Pallas kernels for 9%

profile of v2, /device:TPU:1, one launch (start us, length us, event | category | flops | bytes accessed | tf_op | source)
XLA Modules:
  0.0 439.1 jit_solution(13723973900740936184)
XLA Ops:
  2.0 4.1 merge.14
  6.1 3.4 collective-permute-start.1
  9.5 4.1 merge.13
  14.9 8.2 %all-to-all-start = ((bf16[8,16,3584]{2,1,0:T(8,128)(2,1)}), bf16[8,16,3584]{2,1,0:T(8,128)(2,1)S(1)}, u32[]{:S(2)}, u32[]{:S(2)}) async-start(bf16[8,16,3584]{2,1,0:T(8,128)(2,1)} %copy-done), calls=%async_computation | async-start | bytes 1835008 | tf_op jit(solution)/shard_map/merge/all_to_all | solution.py:387
  23.1 3.4 merge.20
  28.0 3.4 merge.21
  32.2 17.2 %all-to-all-done.x_ref = bf16[8,16,3584]{2,1,0:T(8,128)(2,1)S(1)} async-done(((bf16[8,16,3584]{2,1,0:T(8,128)(2,1)}), bf16[8,16,3584]{2,1,0:T(8,128)(2,1)S(1)}, u32[]{:S(2)}, u32[]{:S(2)}) %all-to-all-start) | async-done | bytes 917536 | tf_op jit(solution)/shard_map/merge/all_to_all | solution.py:387
  49.5 5.1 %collective-permute-done.refs_2_ = bf16[2,2,896,256]{3,2,1,0:T(8,128)(2,1)S(1)} collective-permute-done((bf16[2,2,896,256]{3,2,1,0:T(8,128)(2,1)}, bf16[2,2,896,256]{3,2,1,0:T(8,128)(2,1)S(1)}, u32[]{:S(2)}, u32[]{:S(2)}) %collective-permute-start) | collective-permute-done | bytes 1835040 | tf_op jit(solution)/shard_map/merge/ppermute | solution.py:19
  54.6 3.7 merge.18
  61.2 13.1 %collective-permute-done.19.refs_2_ = bf16[2,2,128,896]{3,2,1,0:T(8,128)(2,1)} collective-permute-done((bf16[2,2,128,896]{3,2,1,0:T(8,128)(2,1)}, bf16[2,2,128,896]{3,2,1,0:T(8,128)(2,1)}, u32[]{:S(2)}, u32[]{:S(2)}) %collective-permute-start.19) | collective-permute-done | bytes 917536 | tf_op jit(solution)/shard_map/merge/ppermute | solution.py:19
  80.4 13.3 %collective-permute-done.6.refs_5_ = bf16[2,1,896,256]{3,2,1,0:T(8,128)(2,1)S(1)} collective-permute-done((bf16[2,1,896,256]{3,2,1,0:T(8,128)(2,1)S(1)}, bf16[2,1,896,256]{3,2,1,0:T(8,128)(2,1)S(1)}, u32[]{:S(2)}, u32[]{:S(2)}) %collective-permute-start.6) | collective-permute-done | bytes 917536 | tf_op jit(solution)/shard_map/merge/ppermute | solution.py:19
  93.8 3.9 merge.19.refs_4_
  97.9 5.5 %collective-permute-start.14 = (bf16[896,256]{1,0:T(8,128)(2,1)S(1)}, bf16[896,256]{1,0:T(8,128)(2,1)S(1)}, u32[]{:S(2)}, u32[]{:S(2)}) collective-permute-start(bf16[896,256]{1,0:T(8,128)(2,1)S(1)} %merge.19.refs_4_), channel_id=1, source_target_pairs={{0,1},{1,0},{2,3},{3,2},{4,5},{5,4},{6,7},{7,6},{8,9},{9,8},{10,11... | collective-permute-start | bytes 1376264 | tf_op jit(solution)/shard_map/merge/ppermute | solution.py:19
  107.6 5.9 %collective-permute-done.7.refs_5_ = bf16[896,256]{1,0:T(8,128)(2,1)S(1)} collective-permute-done((bf16[896,256]{1,0:T(8,128)(2,1)S(1)}, bf16[896,256]{1,0:T(8,128)(2,1)S(1)}, u32[]{:S(2)}, u32[]{:S(2)}) %collective-permute-start.7) | collective-permute-done | bytes 458784 | tf_op jit(solution)/shard_map/merge/ppermute | solution.py:19
  113.5 3.3 collective-permute-start.10
  123.3 3.3 collective-permute-start.17
  126.6 4.0 collective-permute-done.8.refs_6_
  149.7 3.7 collective-permute-done.23.refs_1_
  163.8 9.6 %collective-permute-start.35 = (bf16[128,896]{1,0:T(8,128)(2,1)S(1)}, bf16[128,896]{1,0:T(8,128)(2,1)S(1)}, u32[]{:S(2)}, u32[]{:S(2)}) collective-permute-start(bf16[128,896]{1,0:T(8,128)(2,1)S(1)} %collective-permute-done.28.refs_6_), channel_id=1, source_target_pairs={{0,1},{1,0},{2,3},{3,2},{4,5},{5,4},{6,7},{7,6},{8,9},{9,8},{10,11... | collective-permute-start | bytes 688136 | tf_op jit(solution)/shard_map/merge/ppermute | solution.py:19
  177.3 34.3 %all_to_all.46.p_ref = bf16[8,16,3584]{2,1,0:T(8,128)(2,1)S(1)} all-to-all(bf16[8,16,3584]{2,1,0:T(8,128)(2,1)S(1)} %layer.16), channel_id=1, replica_groups={{0,2,4,6,8,10,12,14},{1,3,5,7,9,11,13,15},{16,18,20,22,24,26,28,30},{17..., dimensions={0} | all-to-all | bytes 1835008 | tf_op jit(solution)/shard_map/layer/all_to_all | solution.py:387
  217.2 27.0 %all_to_all.47.x_ref = bf16[8,16,3584]{2,1,0:T(8,128)(2,1)S(1)} all-to-all(bf16[8,16,3584]{2,1,0:T(8,128)(2,1)S(1)} %layer.18), channel_id=1, replica_groups={{0,2,4,6,8,10,12,14},{1,3,5,7,9,11,13,15},{16,18,20,22,24,26,28,30},{17..., dimensions={0} | all-to-all | bytes 1835008 | tf_op jit(solution)/shard_map/layer/all_to_all | solution.py:387
  251.9 28.8 %all_to_all.48.p_ref = bf16[8,16,3584]{2,1,0:T(8,128)(2,1)S(1)} all-to-all(bf16[8,16,3584]{2,1,0:T(8,128)(2,1)S(1)} %layer.20), channel_id=1, replica_groups={{0,2,4,6,8,10,12,14},{1,3,5,7,9,11,13,15},{16,18,20,22,24,26,28,30},{17..., dimensions={0} | all-to-all | bytes 1835008 | tf_op jit(solution)/shard_map/layer/all_to_all | solution.py:387
  280.9 4.1 collective-permute-start.39
  287.3 27.0 %all_to_all.49.x_ref = bf16[8,16,3584]{2,1,0:T(8,128)(2,1)S(1)} all-to-all(bf16[8,16,3584]{2,1,0:T(8,128)(2,1)S(1)} %layer.22), channel_id=1, replica_groups={{0,2,4,6,8,10,12,14},{1,3,5,7,9,11,13,15},{16,18,20,22,24,26,28,30},{17..., dimensions={0} | all-to-all | bytes 1835008 | tf_op jit(solution)/shard_map/layer/all_to_all | solution.py:387
  321.9 28.8 %all_to_all.50.p_ref = bf16[8,16,3584]{2,1,0:T(8,128)(2,1)S(1)} all-to-all(bf16[8,16,3584]{2,1,0:T(8,128)(2,1)S(1)} %layer.24), channel_id=1, replica_groups={{0,2,4,6,8,10,12,14},{1,3,5,7,9,11,13,15},{16,18,20,22,24,26,28,30},{17..., dimensions={0} | all-to-all | bytes 1835008 | tf_op jit(solution)/shard_map/layer/all_to_all | solution.py:387
  351.0 4.1 collective-permute-start.41
  357.3 27.0 %all_to_all.51.x_ref = bf16[8,16,3584]{2,1,0:T(8,128)(2,1)S(1)} all-to-all(bf16[8,16,3584]{2,1,0:T(8,128)(2,1)S(1)} %layer.26), channel_id=1, replica_groups={{0,2,4,6,8,10,12,14},{1,3,5,7,9,11,13,15},{16,18,20,22,24,26,28,30},{17..., dimensions={0} | all-to-all | bytes 1835008 | tf_op jit(solution)/shard_map/layer/all_to_all | solution.py:387
  389.5 3.4 layer.28
  392.9 3.7 all-to-all-start.7
  396.6 24.0 %all-to-all-done.7.p_ref = bf16[8,16,3584]{2,1,0:T(8,128)(2,1)S(1)} async-done(((bf16[8,16,3584]{2,1,0:T(8,128)(2,1)}), bf16[8,16,3584]{2,1,0:T(8,128)(2,1)S(1)}, u32[]{:S(2)}, u32[]{:S(2)}) %all-to-all-start.7) | async-done | bytes 917536 | tf_op jit(solution)/shard_map/layer/all_to_all | solution.py:387
  423.4 6.1 %all-to-all-start.8 = ((f32[16,1,1]{2,1,0:T(1,128)}), f32[16,1,1]{2,1,0:T(1,128)S(1)}, u32[]{:S(2)}, u32[]{:S(2)}) async-start(f32[16,1,1]{2,1,0:T(1,128)} %broadcast_in_dim.29), calls=%async_computation.8 | async-start | bytes 16384 | tf_op jit(solution)/shard_map/loss/all_to_all | solution.py:436
  429.5 7.0 %all-to-all-done.8 = f32[16,1,1]{2,1,0:T(1,128)S(1)} async-done(((f32[16,1,1]{2,1,0:T(1,128)}), f32[16,1,1]{2,1,0:T(1,128)S(1)}, u32[]{:S(2)}, u32[]{:S(2)}) %all-to-all-start.8) | async-done | bytes 96 | tf_op jit(solution)/shard_map/loss/all_to_all | solution.py:436
  (116 shorter events, 91.7 us)
Async XLA Ops:
  6.1 43.4 %collective-permute-start.1 = (bf16[2,2,896,256]{3,2,1,0:T(8,128)(2,1)}, bf16[2,2,896,256]{3,2,1,0:T(8,128)(2,1)}, u32[]{:S(2)}, u32[]{:S(2)}) collective-permute-start(bf16[2,2,896,256]{3,2,1,0:T(8,128)(2,1)} %merge.14), channel_id=1, source_target_pairs={{0,48},{16,32},{32,16},{48,0},{1,49},{17,33},{33,17},{49,1},{2,50}... | collective-permute-start | bytes 5505032 | tf_op jit(solution)/shard_map/merge/ppermute | solution.py:19
  13.6 41.0 %collective-permute-start = (bf16[2,2,896,256]{3,2,1,0:T(8,128)(2,1)}, bf16[2,2,896,256]{3,2,1,0:T(8,128)(2,1)S(1)}, u32[]{:S(2)}, u32[]{:S(2)}) collective-permute-start(bf16[2,2,896,256]{3,2,1,0:T(8,128)(2,1)} %merge.13), channel_id=1, source_target_pairs={{0,16},{16,0},{32,48},{48,32},{1,17},{17,1},{33,49},{49,33},{2,18}... | collective-permute-start | bytes 5505032 | tf_op jit(solution)/shard_map/merge/ppermute | solution.py:19
  14.9 34.6 %all-to-all-start = ((bf16[8,16,3584]{2,1,0:T(8,128)(2,1)}), bf16[8,16,3584]{2,1,0:T(8,128)(2,1)S(1)}, u32[]{:S(2)}, u32[]{:S(2)}) async-start(bf16[8,16,3584]{2,1,0:T(8,128)(2,1)} %copy-done), calls=%async_computation | async-start | bytes 1835008 | tf_op jit(solution)/shard_map/merge/all_to_all | solution.py:387
  26.5 47.7 %collective-permute-start.19 = (bf16[2,2,128,896]{3,2,1,0:T(8,128)(2,1)}, bf16[2,2,128,896]{3,2,1,0:T(8,128)(2,1)}, u32[]{:S(2)}, u32[]{:S(2)}) collective-permute-start(bf16[2,2,128,896]{3,2,1,0:T(8,128)(2,1)} %merge.20), channel_id=1, source_target_pairs={{0,16},{16,0},{32,48},{48,32},{1,17},{17,1},{33,49},{49,33},{2,18}... | collective-permute-start | bytes 2752520 | tf_op jit(solution)/shard_map/merge/ppermute | solution.py:19
  31.5 42.8 %collective-permute-start.20 = (bf16[2,2,128,896]{3,2,1,0:T(8,128)(2,1)}, bf16[2,2,128,896]{3,2,1,0:T(8,128)(2,1)}, u32[]{:S(2)}, u32[]{:S(2)}) collective-permute-start(bf16[2,2,128,896]{3,2,1,0:T(8,128)(2,1)} %merge.21), channel_id=1, source_target_pairs={{0,48},{16,32},{32,16},{48,0},{1,49},{17,33},{33,17},{49,1},{2,50}... | collective-permute-start | bytes 2752520 | tf_op jit(solution)/shard_map/merge/ppermute | solution.py:19
  58.3 35.5 %collective-permute-start.6 = (bf16[2,1,896,256]{3,2,1,0:T(8,128)(2,1)S(1)}, bf16[2,1,896,256]{3,2,1,0:T(8,128)(2,1)S(1)}, u32[]{:S(2)}, u32[]{:S(2)}) collective-permute-start(bf16[2,1,896,256]{3,2,1,0:T(8,128)(2,1)S(1)} %merge.18), channel_id=1, source_target_pairs={{0,16},{16,0},{32,48},{48,32},{1,17},{17,1},{33,49},{49,33},{2,18}... | collective-permute-start | bytes 2752520 | tf_op jit(solution)/shard_map/merge/ppermute | solution.py:19
  61.1 36.8 %collective-permute-start.2 = (bf16[2,1,896,256]{3,2,1,0:T(8,128)(2,1)S(1)}, bf16[2,1,896,256]{3,2,1,0:T(8,128)(2,1)S(1)}, u32[]{:S(2)}, u32[]{:S(2)}) collective-permute-start(bf16[2,1,896,256]{3,2,1,0:T(8,128)(2,1)S(1)} %merge.16), channel_id=1, source_target_pairs={{0,48},{16,32},{32,16},{48,0},{1,49},{17,33},{33,17},{49,1},{2,50}... | collective-permute-start | bytes 2752520 | tf_op jit(solution)/shard_map/merge/ppermute | solution.py:19
  77.2 29.1 %collective-permute-start.21 = (bf16[2,1,128,896]{3,2,1,0:T(8,128)(2,1)S(1)}, bf16[2,1,128,896]{3,2,1,0:T(8,128)(2,1)S(1)}, u32[]{:S(2)}, u32[]{:S(2)}) collective-permute-start(bf16[2,1,128,896]{3,2,1,0:T(8,128)(2,1)S(1)} %merge.22), channel_id=1, source_target_pairs={{0,48},{16,32},{32,16},{48,0},{1,49},{17,33},{33,17},{49,1},{2,50}... | collective-permute-start | bytes 1376264 | tf_op jit(solution)/shard_map/merge/ppermute | solution.py:19
  80.3 27.0 %collective-permute-start.22 = (bf16[2,1,128,896]{3,2,1,0:T(8,128)(2,1)S(1)}, bf16[2,1,128,896]{3,2,1,0:T(8,128)(2,1)S(1)}, u32[]{:S(2)}, u32[]{:S(2)}) collective-permute-start(bf16[2,1,128,896]{3,2,1,0:T(8,128)(2,1)S(1)} %merge.23), channel_id=1, source_target_pairs={{0,16},{16,0},{32,48},{48,32},{1,17},{17,1},{33,49},{49,33},{2,18}... | collective-permute-start | bytes 1376264 | tf_op jit(solution)/shard_map/merge/ppermute | solution.py:19
  97.7 15.8 %collective-permute-start.7 = (bf16[896,256]{1,0:T(8,128)(2,1)S(1)}, bf16[896,256]{1,0:T(8,128)(2,1)S(1)}, u32[]{:S(2)}, u32[]{:S(2)}) collective-permute-start(bf16[896,256]{1,0:T(8,128)(2,1)S(1)} %merge.19.refs_4_), channel_id=1, source_target_pairs={{0,16},{16,0},{32,48},{48,32},{1,17},{17,1},{33,49},{49,33},{2,18}... | collective-permute-start | bytes 1376264 | tf_op jit(solution)/shard_map/merge/ppermute | solution.py:19
  97.9 18.9 %collective-permute-start.9 = (bf16[896,256]{1,0:T(8,128)(2,1)S(1)}, bf16[896,256]{1,0:T(8,128)(2,1)S(1)}, u32[]{:S(2)}, u32[]{:S(2)}) collective-permute-start(bf16[896,256]{1,0:T(8,128)(2,1)S(1)} %merge.19.refs_4_), channel_id=1, source_target_pairs={{0,48},{16,32},{32,16},{48,0},{1,49},{17,33},{33,17},{49,1},{2,50}... | collective-permute-start | bytes 1376264 | tf_op jit(solution)/shard_map/merge/ppermute | solution.py:19
  97.9 20.6 %collective-permute-start.14 = (bf16[896,256]{1,0:T(8,128)(2,1)S(1)}, bf16[896,256]{1,0:T(8,128)(2,1)S(1)}, u32[]{:S(2)}, u32[]{:S(2)}) collective-permute-start(bf16[896,256]{1,0:T(8,128)(2,1)S(1)} %merge.19.refs_4_), channel_id=1, source_target_pairs={{0,1},{1,0},{2,3},{3,2},{4,5},{5,4},{6,7},{7,6},{8,9},{9,8},{10,11... | collective-permute-start | bytes 1376264 | tf_op jit(solution)/shard_map/merge/ppermute | solution.py:19
  106.3 13.9 %collective-permute-start.4 = (bf16[896,256]{1,0:T(8,128)(2,1)S(1)}, bf16[896,256]{1,0:T(8,128)(2,1)S(1)}, u32[]{:S(2)}, u32[]{:S(2)}) collective-permute-start(bf16[896,256]{1,0:T(8,128)(2,1)S(1)} %merge.17.refs_0_), channel_id=1, source_target_pairs={{0,48},{16,32},{32,16},{48,0},{1,49},{17,33},{33,17},{49,1},{2,50}... | collective-permute-start | bytes 1376264 | tf_op jit(solution)/shard_map/merge/ppermute | solution.py:19
  107.3 16.0 %collective-permute-start.3 = (bf16[896,256]{1,0:T(8,128)(2,1)S(1)}, bf16[896,256]{1,0:T(8,128)(2,1)S(1)}, u32[]{:S(2)}, u32[]{:S(2)}) collective-permute-start(bf16[896,256]{1,0:T(8,128)(2,1)S(1)} %merge.17.refs_0_), channel_id=1, source_target_pairs={{0,16},{16,0},{32,48},{48,32},{1,17},{17,1},{33,49},{49,33},{2,18}... | collective-permute-start | bytes 1376264 | tf_op jit(solution)/shard_map/merge/ppermute | solution.py:19
  113.5 13.2 %collective-permute-start.10 = (bf16[896,256]{1,0:T(8,128)(2,1)S(1)}, bf16[896,256]{1,0:T(8,128)(2,1)S(1)}, u32[]{:S(2)}, u32[]{:S(2)}) collective-permute-start(bf16[896,256]{1,0:T(8,128)(2,1)S(1)} %merge.17.refs_0_), channel_id=1, source_target_pairs={{0,1},{1,0},{2,3},{3,2},{4,5},{5,4},{6,7},{7,6},{8,9},{9,8},{10,11... | collective-permute-start | bytes 1376264 | tf_op jit(solution)/shard_map/merge/ppermute | solution.py:19
  116.8 13.8 %collective-permute-start.8 = (bf16[896,256]{1,0:T(8,128)(2,1)S(1)}, bf16[896,256]{1,0:T(8,128)(2,1)S(1)}, u32[]{:S(2)}, u32[]{:S(2)}) collective-permute-start(bf16[896,256]{1,0:T(8,128)(2,1)S(1)} %collective-permute-done.7.refs_5_), channel_id=1, source_target_pairs={{0,48},{16,32},{32,16},{48,0},{1,49},{17,33},{33,17},{49,1},{2,50}... | collective-permute-start | bytes 1376264 | tf_op jit(solution)/shard_map/merge/ppermute | solution.py:19
  118.5 13.5 %collective-permute-start.15 = (bf16[896,256]{1,0:T(8,128)(2,1)S(1)}, bf16[896,256]{1,0:T(8,128)(2,1)S(1)}, u32[]{:S(2)}, u32[]{:S(2)}) collective-permute-start(bf16[896,256]{1,0:T(8,128)(2,1)S(1)} %collective-permute-done.7.refs_5_), channel_id=1, source_target_pairs={{0,1},{1,0},{2,3},{3,2},{4,5},{5,4},{6,7},{7,6},{8,9},{9,8},{10,11... | collective-permute-start | bytes 1376264 | tf_op jit(solution)/shard_map/merge/ppermute | solution.py:19
  120.2 12.9 %collective-permute-start.5 = (bf16[896,256]{1,0:T(8,128)(2,1)S(1)}, bf16[896,256]{1,0:T(8,128)(2,1)S(1)}, u32[]{:S(2)}, u32[]{:S(2)}) collective-permute-start(bf16[896,256]{1,0:T(8,128)(2,1)S(1)} %collective-permute-done.4.refs_3_), channel_id=1, source_target_pairs={{0,16},{16,0},{32,48},{48,32},{1,17},{17,1},{33,49},{49,33},{2,18}... | collective-permute-start | bytes 1376264 | tf_op jit(solution)/shard_map/merge/ppermute | solution.py:19
  123.3 17.9 %collective-permute-start.17 = (bf16[896,256]{1,0:T(8,128)(2,1)S(1)}, bf16[896,256]{1,0:T(8,128)(2,1)S(1)}, u32[]{:S(2)}, u32[]{:S(2)}) collective-permute-start(bf16[896,256]{1,0:T(8,128)(2,1)S(1)} %collective-permute-done.9.refs_7_), channel_id=1, source_target_pairs={{0,1},{1,0},{2,3},{3,2},{4,5},{5,4},{6,7},{7,6},{8,9},{9,8},{10,11... | collective-permute-start | bytes 1376264 | tf_op jit(solution)/shard_map/merge/ppermute | solution.py:19
  126.6 14.6 %collective-permute-start.11 = (bf16[896,256]{1,0:T(8,128)(2,1)S(1)}, bf16[896,256]{1,0:T(8,128)(2,1)S(1)}, u32[]{:S(2)}, u32[]{:S(2)}) collective-permute-start(bf16[896,256]{1,0:T(8,128)(2,1)S(1)} %collective-permute-done.3.refs_1_), channel_id=1, source_target_pairs={{0,1},{1,0},{2,3},{3,2},{4,5},{5,4},{6,7},{7,6},{8,9},{9,8},{10,11... | collective-permute-start | bytes 1376264 | tf_op jit(solution)/shard_map/merge/ppermute | solution.py:19
  130.6 11.5 %collective-permute-start.13 = (bf16[896,256]{1,0:T(8,128)(2,1)S(1)}, bf16[896,256]{1,0:T(8,128)(2,1)S(1)}, u32[]{:S(2)}, u32[]{:S(2)}) collective-permute-start(bf16[896,256]{1,0:T(8,128)(2,1)S(1)} %collective-permute-done.4.refs_3_), channel_id=1, source_target_pairs={{0,1},{1,0},{2,3},{3,2},{4,5},{5,4},{6,7},{7,6},{8,9},{9,8},{10,11... | collective-permute-start | bytes 1376264 | tf_op jit(solution)/shard_map/merge/ppermute | solution.py:19
  133.1 11.7 %collective-permute-start.12 = (bf16[896,256]{1,0:T(8,128)(2,1)S(1)}, bf16[896,256]{1,0:T(8,128)(2,1)S(1)}, u32[]{:S(2)}, u32[]{:S(2)}) collective-permute-start(bf16[896,256]{1,0:T(8,128)(2,1)S(1)} %collective-permute-done.5.refs_2_), channel_id=1, source_target_pairs={{0,1},{1,0},{2,3},{3,2},{4,5},{5,4},{6,7},{7,6},{8,9},{9,8},{10,11... | collective-permute-start | bytes 1376264 | tf_op jit(solution)/shard_map/merge/ppermute | solution.py:19
  142.1 11.3 %collective-permute-start.23 = (bf16[128,896]{1,0:T(8,128)(2,1)S(1)}, bf16[128,896]{1,0:T(8,128)(2,1)S(1)}, u32[]{:S(2)}, u32[]{:S(2)}) collective-permute-start(bf16[128,896]{1,0:T(8,128)(2,1)S(1)} %merge.24.refs_0_), channel_id=1, source_target_pairs={{0,16},{16,0},{32,48},{48,32},{1,17},{17,1},{33,49},{49,33},{2,18}... | collective-permute-start | bytes 688136 | tf_op jit(solution)/shard_map/merge/ppermute | solution.py:19
  142.8 11.7 %collective-permute-start.25 = (bf16[128,896]{1,0:T(8,128)(2,1)S(1)}, bf16[128,896]{1,0:T(8,128)(2,1)S(1)}, u32[]{:S(2)}, u32[]{:S(2)}) collective-permute-start(bf16[128,896]{1,0:T(8,128)(2,1)S(1)} %merge.24.refs_0_), channel_id=1, source_target_pairs={{0,48},{16,32},{32,16},{48,0},{1,49},{17,33},{33,17},{49,1},{2,50}... | collective-permute-start | bytes 688136 | tf_op jit(solution)/shard_map/merge/ppermute | solution.py:19
  144.8 12.0 %collective-permute-start.33 = (bf16[128,896]{1,0:T(8,128)(2,1)S(1)}, bf16[128,896]{1,0:T(8,128)(2,1)S(1)}, u32[]{:S(2)}, u32[]{:S(2)}) collective-permute-start(bf16[128,896]{1,0:T(8,128)(2,1)S(1)} %merge.25.refs_4_), channel_id=1, source_target_pairs={{0,1},{1,0},{2,3},{3,2},{4,5},{5,4},{6,7},{7,6},{8,9},{9,8},{10,11... | collective-permute-start | bytes 688136 | tf_op jit(solution)/shard_map/merge/ppermute | solution.py:19
  156.8 16.6 %collective-permute-start.32 = (bf16[128,896]{1,0:T(8,128)(2,1)S(1)}, bf16[128,896]{1,0:T(8,128)(2,1)S(1)}, u32[]{:S(2)}, u32[]{:S(2)}) collective-permute-start(bf16[128,896]{1,0:T(8,128)(2,1)S(1)} %collective-permute-done.25.refs_3_), channel_id=1, source_target_pairs={{0,1},{1,0},{2,3},{3,2},{4,5},{5,4},{6,7},{7,6},{8,9},{9,8},{10,11... | collective-permute-start | bytes 688136 | tf_op jit(solution)/shard_map/merge/ppermute | solution.py:19
  158.2 15.2 %collective-permute-start.34 = (bf16[128,896]{1,0:T(8,128)(2,1)S(1)}, bf16[128,896]{1,0:T(8,128)(2,1)S(1)}, u32[]{:S(2)}, u32[]{:S(2)}) collective-permute-start(bf16[128,896]{1,0:T(8,128)(2,1)S(1)} %collective-permute-done.24.refs_5_), channel_id=1, source_target_pairs={{0,1},{1,0},{2,3},{3,2},{4,5},{5,4},{6,7},{7,6},{8,9},{9,8},{10,11... | collective-permute-start | bytes 688136 | tf_op jit(solution)/shard_map/merge/ppermute | solution.py:19
  160.6 12.8 %collective-permute-start.36 = (bf16[128,896]{1,0:T(8,128)(2,1)S(1)}, bf16[128,896]{1,0:T(8,128)(2,1)S(1)}, u32[]{:S(2)}, u32[]{:S(2)}) collective-permute-start(bf16[128,896]{1,0:T(8,128)(2,1)S(1)} %collective-permute-done.26.refs_7_), channel_id=1, source_target_pairs={{0,1},{1,0},{2,3},{3,2},{4,5},{5,4},{6,7},{7,6},{8,9},{9,8},{10,11... | collective-permute-start | bytes 688136 | tf_op jit(solution)/shard_map/merge/ppermute | solution.py:19
  162.5 10.9 %collective-permute-start.31 = (bf16[128,896]{1,0:T(8,128)(2,1)S(1)}, bf16[128,896]{1,0:T(8,128)(2,1)S(1)}, u32[]{:S(2)}, u32[]{:S(2)}) collective-permute-start(bf16[128,896]{1,0:T(8,128)(2,1)S(1)} %collective-permute-done.27.refs_2_), channel_id=1, source_target_pairs={{0,1},{1,0},{2,3},{3,2},{4,5},{5,4},{6,7},{7,6},{8,9},{9,8},{10,11... | collective-permute-start | bytes 688136 | tf_op jit(solution)/shard_map/merge/ppermute | solution.py:19
  163.8 11.1 %collective-permute-start.35 = (bf16[128,896]{1,0:T(8,128)(2,1)S(1)}, bf16[128,896]{1,0:T(8,128)(2,1)S(1)}, u32[]{:S(2)}, u32[]{:S(2)}) collective-permute-start(bf16[128,896]{1,0:T(8,128)(2,1)S(1)} %collective-permute-done.28.refs_6_), channel_id=1, source_target_pairs={{0,1},{1,0},{2,3},{3,2},{4,5},{5,4},{6,7},{7,6},{8,9},{9,8},{10,11... | collective-permute-start | bytes 688136 | tf_op jit(solution)/shard_map/merge/ppermute | solution.py:19
  392.9 27.7 %all-to-all-start.7 = ((bf16[8,16,3584]{2,1,0:T(8,128)(2,1)}), bf16[8,16,3584]{2,1,0:T(8,128)(2,1)S(1)}, u32[]{:S(2)}, u32[]{:S(2)}) async-start(bf16[8,16,3584]{2,1,0:T(8,128)(2,1)} %layer.28), calls=%async_computation.7 | async-start | bytes 1835008 | tf_op jit(solution)/shard_map/layer/all_to_all | solution.py:387
  423.4 13.1 %all-to-all-start.8 = ((f32[16,1,1]{2,1,0:T(1,128)}), f32[16,1,1]{2,1,0:T(1,128)S(1)}, u32[]{:S(2)}, u32[]{:S(2)}) async-start(f32[16,1,1]{2,1,0:T(1,128)} %broadcast_in_dim.29), calls=%async_computation.8 | async-start | bytes 16384 | tf_op jit(solution)/shard_map/loss/all_to_all | solution.py:436
  (18 other events, 123.5 us)
